TPU v7x, 32 devices: a whole 2x2x4 slice. The times are simulated.
32 devices in a mesh: dp: 8 (over z, y), mp: 4 (over x, core).
Axes of the slice: x: 2, y: 2, z: 4, core: 2. Of those that a mesh axis runs over, the one named last changes fastest.
Arguments:
- hidden: bfloat16 [4096, 8192], P('dp', 'mp'), may hold values from -64 to 64
- queries: bfloat16 [4096, 4096], P('dp', 'mp'), may hold values from -512 to 512
- upstream: bfloat16 [4096, 4096], P('dp', 'mp'), may hold values from -6 to 6
- key_weight: bfloat16 [8192, 512], P(None, 'mp'), may hold values from -1 to 1
- value_weight: bfloat16 [8192, 512], P(None, 'mp'), may hold values from -0.0625 to 0.0625
- lengths: int32 [8, 8], replicated, may hold values from 0 to 64, as said below
- advantage: float32 [8, 8], replicated, may hold values from -4 to 4
Outputs:
- attention_out: bfloat16 [2048, 4096], P('dp', 'mp')
- key_grad: float32 [8192, 512], P('dp', 'mp')
- value_grad: float32 [8192, 512], P('dp', 'mp')
Inputs may be any that keep to these rules, and one draw needn't show every extreme that they name: `lengths`: each rollout device fills its slots from slot 0; a used slot holds 33 to 64 tokens, later slots hold 0. Devices come in aligned groups of four; in each, the second or the third device is heavy and uses 6 to 8 slots; every other device uses one slot plus one for each neighbour that exists and is not heavy. One device's responses total at most 512 tokens and some device holds exactly 512; under the learner rule a learner receives at most 256 tokens and some learner exactly 256, and at most 128 tokens go from one device to one neighbour, exactly 128 from some device.
All inputs are finite; a program needn't handle non-finite values.
Results may differ from a plain program's by a relative error of at most 0.0082.
Values may be sent and summed in bfloat16 or wider, within the bound.
A program may use at most 128 MiB of HBM per device.

v0:
```python
import jax
import jax.numpy as jnp
from jax import lax
from jax.sharding import PartitionSpec as P

HD = 128
LMAX = 64
CAP_R = 512
CAP_L = 256
PIECE = 128


epsilon = 1e-06
masked_score = -1e30


def passed_along(value, axis, steps):
    count = lax.axis_size(axis)
    first, last = (max(0, -steps), min(count, count - steps))
    return lax.ppermute(value, axis, [(source, source + steps) for source in range(first, last)])


def derive_learner(lengths):
    device_total = lengths.shape[0]
    slot_total = lengths.shape[1]
    used_slots = jnp.sum((lengths > 0).astype(jnp.int32), axis=1)
    heavy_flag = used_slots >= 6
    devices = jnp.arange(device_total, dtype=jnp.int32)
    left_heavy = jnp.concatenate([jnp.zeros((1,), bool), heavy_flag[:-1]])
    light_left = ((devices > 0) & jnp.logical_not(left_heavy)).astype(jnp.int32)
    sent_left = jnp.where(heavy_flag, (used_slots - 4) // 2, light_left)
    kept_count = jnp.where(heavy_flag, 4, 1).astype(jnp.int32)
    slot_ids = jnp.arange(slot_total, dtype=jnp.int32)[None, :]
    slot_moves = jnp.where(
        slot_ids < sent_left[:, None],
        -1,
        jnp.where(
            slot_ids < (sent_left + kept_count)[:, None],
            0,
            jnp.where(slot_ids < used_slots[:, None], 1, 0),
        ),
    )
    return devices[:, None] + slot_moves


def pick_entry(table, index):
    return lax.dynamic_index_in_dim(table, index, 0, keepdims=False)


def extend_rows(array):
    return jnp.concatenate([array, jnp.zeros((1,) + array.shape[1:], array.dtype)], axis=0)


def device_counts(lengths, learner):
    devices = jnp.arange(lengths.shape[0], dtype=jnp.int32)[:, None]
    toward_prev = jnp.sum(jnp.where(learner == devices - 1, lengths, 0), axis=1)
    staying = jnp.sum(jnp.where(learner == devices, lengths, 0), axis=1)
    toward_later = jnp.sum(jnp.where(learner == devices + 1, lengths, 0), axis=1)
    return (toward_prev, staying, toward_later)


def row_labels(lengths, advantage, device, positions):
    slot_lengths = pick_entry(lengths, device)
    slot_ends = jnp.cumsum(slot_lengths)
    slots = jnp.sum((positions[:, None] >= slot_ends[None, :]).astype(jnp.int32), axis=1)
    inside = (positions >= 0) & (positions < slot_ends[-1])
    rates = pick_entry(advantage, device) / jnp.maximum(slot_lengths, 1).astype(jnp.float32)
    matches = (
        slots[:, None] == jnp.arange(slot_lengths.shape[0], dtype=jnp.int32)[None, :]
    ) & inside[:, None]
    scales = jnp.sum(jnp.where(matches, rates[None, :], 0.0), axis=1)
    segments = jnp.where(inside, device * slot_lengths.shape[0] + slots, -1)
    return (segments, scales)


def layer_pass(hidden_rows, query_rows, upstream_rows, segments, scales, key_weight, value_weight):
    full_rows = lax.all_gather(hidden_rows, "mp", axis=1, tiled=True)
    widened = full_rows.astype(jnp.float32)
    normed = (
        widened * lax.rsqrt(jnp.mean(widened * widened, axis=1, keepdims=True) + epsilon)
    ).astype(jnp.bfloat16)
    key_rows = jnp.dot(normed, key_weight, preferred_element_type=jnp.float32).astype(jnp.bfloat16)
    value_rows = jnp.dot(normed, value_weight, preferred_element_type=jnp.float32).astype(
        jnp.bfloat16
    )
    row_count = normed.shape[0]
    kv_heads = key_weight.shape[1] // HD
    group_size = query_rows.shape[1] // HD // kv_heads
    inverse_root = HD ** (-0.5)
    cotangent = (scales[:, None] * upstream_rows.astype(jnp.float32)).astype(jnp.bfloat16)
    window_total = 2 * row_count // LMAX
    positions = jnp.arange(row_count, dtype=jnp.int32)
    offsets = jnp.arange(LMAX, dtype=jnp.int32)
    earlier_seg = jnp.concatenate([jnp.full((1,), -2, jnp.int32), segments[:-1]])
    opening = (segments >= 0) & (segments != earlier_seg)
    rank = jnp.cumsum(opening.astype(jnp.int32)) - 1
    window_ids = jnp.arange(window_total, dtype=jnp.int32)
    start_hit = opening[None, :] & (rank[None, :] == window_ids[:, None])
    window_start = jnp.sum(jnp.where(start_hit, positions[None, :], 0), axis=1)
    window_seg = jnp.sum(jnp.where(start_hit, segments[None, :], 0), axis=1)
    present = jnp.any(start_hit, axis=1)
    raw_index = window_start[:, None] + offsets[None, :]
    index = jnp.clip(raw_index, 0, row_count - 1)
    valid = present[:, None] & (raw_index < row_count) & (segments[index] == window_seg[:, None])
    query_win = query_rows[index].reshape(window_total, LMAX, kv_heads, group_size, HD)
    key_win = key_rows[index].reshape(window_total, LMAX, kv_heads, HD)
    value_win = value_rows[index].reshape(window_total, LMAX, kv_heads, HD)
    cot_win = jnp.where(valid[:, :, None], cotangent[index], jnp.zeros((), jnp.bfloat16))
    cot_win = cot_win.reshape(window_total, LMAX, kv_heads, group_size, HD)
    allowed = (offsets[None, :] <= offsets[:, None])[None, :, :] & valid[:, None, :]
    scores = (
        jnp.einsum("wtkgd,wukd->wkgtu", query_win, key_win, preferred_element_type=jnp.float32)
        * inverse_root
    )
    scores = jnp.where(allowed[:, None, None, :, :], scores, masked_score)
    row_peak = jnp.max(scores, axis=-1, keepdims=True)
    raised = jnp.exp(scores - row_peak)
    probability = raised / jnp.sum(raised, axis=-1, keepdims=True)
    weights = probability.astype(jnp.bfloat16)
    attended_win = jnp.einsum(
        "wkgtu,wukd->wtkgd", weights, value_win, preferred_element_type=jnp.float32
    ).astype(jnp.bfloat16)
    prob_grad = jnp.einsum(
        "wtkgd,wukd->wkgtu", cot_win, value_win, preferred_element_type=jnp.float32
    )
    centre = jnp.sum(probability * prob_grad, axis=-1, keepdims=True)
    score_grad = (probability * (prob_grad - centre)).astype(jnp.bfloat16)
    key_win_cot = (
        jnp.einsum("wkgtu,wtkgd->wukd", score_grad, query_win, preferred_element_type=jnp.float32)
        * inverse_root
    ).astype(jnp.bfloat16)
    value_win_cot = jnp.einsum(
        "wkgtu,wtkgd->wukd", weights, cot_win, preferred_element_type=jnp.float32
    ).astype(jnp.bfloat16)
    row_window = jnp.clip(rank, 0, window_total - 1)
    row_offset = jnp.clip(positions - window_start[row_window], 0, LMAX - 1)
    flat_index = row_window * LMAX + row_offset
    live = (segments >= 0)[:, None]
    zero_value = jnp.zeros((), jnp.bfloat16)
    attended = jnp.where(
        live,
        attended_win.reshape(window_total * LMAX, kv_heads * group_size * HD)[flat_index],
        zero_value,
    )
    key_cot = jnp.where(
        live, key_win_cot.reshape(window_total * LMAX, kv_heads * HD)[flat_index], zero_value
    )
    value_cot = jnp.where(
        live, value_win_cot.reshape(window_total * LMAX, kv_heads * HD)[flat_index], zero_value
    )
    return (attended, normed, key_cot, value_cot)


def make_term(normed, cots):
    return lax.dot_general(
        normed, cots, (((0,), (0,)), ((), ())), preferred_element_type=jnp.float32
    )


def body(hidden, queries, upstream, key_weight, value_weight, lengths, advantage):
    device = lax.axis_index("dp")
    learner = derive_learner(lengths)
    toward_prev, staying, toward_later = device_counts(lengths, learner)
    zero_entry = jnp.zeros((1,), jnp.int32)
    from_left = pick_entry(jnp.concatenate([zero_entry, toward_later[:-1]]), device)
    own_total = pick_entry(staying, device)
    from_right = pick_entry(jnp.concatenate([toward_prev[1:], zero_entry]), device)
    own_first = pick_entry(toward_prev, device)
    slots_here = jnp.arange(CAP_L, dtype=jnp.int32)
    in_left = slots_here < from_left
    in_own = (slots_here >= from_left) & (slots_here < from_left + own_total)
    in_right = (slots_here >= from_left + own_total) & (
        slots_here < from_left + own_total + from_right
    )
    pool_index = jnp.where(
        in_left,
        slots_here,
        jnp.where(
            in_own,
            PIECE + own_first + slots_here - from_left,
            jnp.where(
                in_right, PIECE + CAP_R + slots_here - from_left - own_total, 2 * PIECE + CAP_R
            ),
        ),
    )
    piece_slots = jnp.arange(PIECE, dtype=jnp.int32)
    send_later = jnp.where(
        piece_slots < pick_entry(toward_later, device), own_first + own_total + piece_slots, CAP_R
    )
    send_prev = jnp.where(piece_slots < own_first, piece_slots, CAP_R)
    rollout_seg, rollout_scale = row_labels(
        lengths, advantage, device, jnp.arange(CAP_R, dtype=jnp.int32)
    )
    attended, normed, key_cot, value_cot = layer_pass(
        hidden, queries, upstream, rollout_seg, rollout_scale, key_weight, value_weight
    )
    attended_ext = extend_rows(attended)
    got_left = passed_along(jnp.take(attended_ext, send_later, axis=0), "dp", 1)
    got_right = passed_along(jnp.take(attended_ext, send_prev, axis=0), "dp", -1)
    pool = jnp.concatenate(
        [got_left, attended, got_right, jnp.zeros((1, attended.shape[1]), attended.dtype)], axis=0
    )
    attention_out = jnp.take(pool, pool_index, axis=0)
    joined = jnp.concatenate([key_cot, value_cot], axis=1)
    summed = lax.psum_scatter(make_term(normed, joined), "dp", scatter_dimension=0, tiled=True)
    key_grad = summed[:, : key_cot.shape[1]]
    value_grad = summed[:, key_cot.shape[1] :]
    return (attention_out, key_grad, value_grad)


def solution(mesh):
    in_specs = (P("dp", "mp"), P("dp", "mp"), P("dp", "mp"), P(None, "mp"), P(None, "mp"), P(), P())
    out_specs = (P("dp", "mp"), P("dp", "mp"), P("dp", "mp"))
    return jax.shard_map(body, mesh=mesh, in_specs=in_specs, out_specs=out_specs, check_vma=False)
```

profile of v0, /device:TPU:0, one launch (start us, length us, event | category | flops | bytes accessed | tf_op | source)
XLA Modules:
  0.0 289.2 jit_solution(11856581051239844870)
XLA Ops:
  7.2 0.7 all-gather.2.cloned.1.call-update
  8.0 0.7 fusion.48
  8.7 0.2 reduce-window.11
  8.8 0.6 slice.32
  9.5 0.7 broadcast_compare_fusion
  10.2 0.7 fusion.41
  10.9 0.3 reduce-window.14
  11.9 6.9 %gather_fusion.1 = s32[1024]{0:T(1024)S(1)} fusion(s32[512]{0:T(512)S(1)} %get-tuple-element.23, s32[1024]{0:T(1024)S(1)} %broadcast_clamp_fusion), kind=kCustom, calls=%fused_computation.3 | custom fusion | bytes 12288 | tf_op jit(solution)/shard_map/gather | solution.py:104
  18.8 5.4 %gather_fusion.3 = bf16[1024,1024]{1,0:T(8,128)(2,1)} fusion(bf16[512,1024]{1,0:T(8,128)(2,1)S(1)} %copy-done.1, s32[1024]{0:T(1024)S(1)} %broadcast_clamp_fusion), kind=kCustom, calls=%fused_computation.5 | custom fusion | bytes 4198400 | tf_op jit(solution)/shard_map/gather | solution.py:105
  24.1 3.8 %copy.29 = bf16[128,8,8,128]{3,2,1,0:T(8,128)(2,1)} copy(bf16[128,8,8,128]{3,1,2,0:T(8,128)(2,1)} %bitcast.162) | data formatting | bytes 4194304
  28.0 0.7 fusion.47
  28.8 1.5 multiply_convert_fusion
  30.3 5.4 %gather_fusion.6 = bf16[1024,1024]{1,0:T(8,128)(2,1)} fusion(bf16[512,1024]{1,0:T(8,128)(2,1)S(1)} %multiply_convert_fusion, s32[1024]{0:T(1024)S(1)} %broadcast_clamp_fusion), kind=kCustom, calls=%fused_computation.8 | custom fusion | bytes 4198400 | tf_op jit(solution)/shard_map/gather | solution.py:108
  35.6 3.6 %copy.31 = bf16[128,8,8,128]{3,2,1,0:T(8,128)(2,1)} copy(bf16[128,8,8,128]{3,1,2,0:T(8,128)(2,1)} %bitcast.161) | data formatting | bytes 4194304
  39.2 0.7 fusion.60
  39.9 4.3 %compare_select_fusion.3 = (s32[512,1]{0,1:T(1,128)S(1)}, s32[512,1]{0,1:T(1,128)S(1)}) fusion(s32[]{:T(128)} %bitcast.32, s32[]{:T(128)} %bitcast.33, s32[]{:T(128)} %bitcast.34, s32[]{:T(128)} %bitcast.35, s32[]{:T(128)} %bitcast.36, s32[]{:T(128)} %bitcast.38, s32[]{:T(128)} %bitcast.37, s32[512,1]{0,1:T(1,128)S(1)} %bitcast.171), kind=kLoop, calls=%fused_computation.85 | loop fusion | flops 7680 | bytes 6172 | tf_op jit(solution)/shard_map/gather | solution.py:136
  44.3 5.7 %select_select_fusion = s32[512]{0:T(512)S(1)} fusion(pred[512]{0:T(512)(128)(4,1)S(1)} %get-tuple-element.17, pred[512]{0:T(512)(128)(4,1)S(1)} %get-tuple-element.16, pred[512]{0:T(512)(128)(4,1)S(1)} %get-tuple-element.15, pred[512]{0:T(512)(128)(4,1)S(1)} %get-tuple-element.14, pred[512]{0:T(512)(128)(4,1)S(1)} %get-tuple-element.13, ...), kind=kLoop, calls=%fused_computation.116 | loop fusion | flops 4608 | bytes 8740 | tf_op jit(solution)/shard_map/gather | solution.py:136
  50.3 0.2 broadcast_and_fusion
  50.5 20.1 %all-gather.2.cloned.1.call-done = bf16[512,8192]{1,0:T(8,128)(2,1)} async-done(((bf16[512,2048]{1,0:T(8,128)(2,1)}), bf16[512,8192]{1,0:T(8,128)(2,1)}) %all-gather.2.cloned.1.call-update) | async-done | bytes 8388624 | tf_op jit(solution)/shard_map/all_gather | solution.py:77
  70.6 5.3 %fusion = f32[512]{0:T(512)S(1)} fusion(bf16[512,8192]{1,0:T(8,128)(2,1)} %all-gather.2.cloned.1.call-done), kind=kLoop, calls=%fused_computation.13 | loop fusion | flops 12582400 | bytes 8390656 | tf_op jit(solution)/shard_map/reduce_sum | solution.py:80
  75.9 0.5 copy-done.4
  76.4 2.4 convolution_convert_fusion
  78.8 3.2 %gather_fusion.2 = bf16[1024,128]{1,0:T(8,128)(2,1)S(1)} fusion(bf16[512,128]{1,0:T(8,128)(2,1)S(1)} %convolution_convert_fusion, s32[1024]{0:T(1024)S(1)} %broadcast_clamp_fusion), kind=kCustom, calls=%fused_computation.4 | custom fusion | bytes 528384 | tf_op jit(solution)/shard_map/gather | solution.py:106
  82.0 6.4 %convolution_convert_fusion.1 = bf16[512,128]{1,0:T(8,128)(2,1)S(1)} fusion(bf16[8192,128]{1,0:T(8,128)(2,1)} %param.13, bf16[512,8192]{1,0:T(8,128)(2,1)} %all-gather.2.cloned.1.call-done, f32[512]{0:T(512)S(1)} %add_rsqrt_fusion), kind=kOutput, calls=%fused_computation.45 | convolution fusion | flops 1086390272 | bytes 10618880 | tf_op jit(solution)/shard_map/dot_general | solution.py:83
  88.4 3.4 %gather_fusion = bf16[1024,128]{1,0:T(8,128)(2,1)S(1)} fusion(bf16[512,128]{1,0:T(8,128)(2,1)S(1)} %convolution_convert_fusion.1, s32[1024]{0:T(1024)S(1)} %broadcast_clamp_fusion), kind=kCustom, calls=%fused_computation.2 | custom fusion | bytes 528384 | tf_op jit(solution)/shard_map/gather | solution.py:107
  91.8 3.9 %fusion.7 = (f32[16,8,64]{2,1,0:T(8,128)S(1)}, f32[16,64,64,8]{2,1,3,0:T(8,128)S(1)}) fusion(pred[16,64,64]{1,2,0:T(8,128)(4,1)S(1)} %broadcast_and_fusion, bf16[16,64,128,1]{2,1,3,0:T(8,128)(2,1)S(1)} %bitcast.168, bf16[16,64,8,128]{3,2,1,0:T(8,128)(2,1)} %bitcast.159), kind=kOutput, calls=%fused_computation.24 | convolution fusion | flops 135782400 | bytes 4554752 | tf_op jit(solution)/shard_map/wtkgd,wukd->wkgtu/dot_general | solution.py:112
  95.7 1.5 fusion.6
  97.2 1.7 fusion.23
  98.9 2.9 %fusion.2 = (f32[16,8,64]{2,1,0:T(8,128)S(1)}, f32[16,64,64,8]{2,1,3,0:T(8,128)S(1)}) fusion(f32[16,8,64]{2,1,0:T(8,128)S(1)} %fusion.6, f32[16,8,64]{2,1,0:T(8,128)S(1)} %get-tuple-element.48, f32[16,64,64,8]{2,1,3,0:T(8,128)S(1)} %get-tuple-element.49, pred[16,64,64]{1,2,0:T(8,128)(4,1)S(1)} %broadcast_and_fusion, ...), kind=kOutput, calls=%fused_computation.18 | convolution fusion | flops 138403840 | bytes 6718464 | tf_op jit(solution)/shard_map/wtkgd,wukd->wkgtu/dot_general | solution.py:123
  101.9 3.3 %fusion.8 = bf16[16,8,64,64]{2,3,1,0:T(8,128)(2,1)} fusion(f32[16,64,64,8]{2,1,3,0:T(8,128)S(1)} %get-tuple-element.51, f32[16,8,64]{2,1,0:T(8,128)S(1)} %get-tuple-element.50, f32[16,8,64]{2,1,0:T(8,128)S(1)} %fusion.6, f32[16,8,64]{2,1,0:T(8,128)S(1)} %get-tuple-element.48, f32[16,64,64,8]{2,1,3,0:T(8,128)S(1)} %get-tuple-element.49, ...), kind=kLoop, calls=%fused_computation.25 | loop fusion | flops 3670016 | bytes 5406720 | tf_op jit(solution)/shard_map/reshape.39
  105.1 4.1 %copy.23 = bf16[16,8,64,64]{3,1,2,0:T(8,128)(2,1)} copy(bf16[16,8,64,64]{2,3,1,0:T(8,128)(2,1)} %fusion.8) | data formatting | bytes 2097152 | tf_op jit(solution)/shard_map/reshape.39
  109.3 1.3 gather_fusion.8
  110.6 3.0 %fusion.26 = bf16[16,128,64]{1,2,0:T(8,128)(2,1)S(1)} fusion(bf16[16,8,64,64]{3,1,2,0:T(8,128)(2,1)} %copy.23, bf16[16,64,8,128]{3,2,1,0:T(8,128)(2,1)} %bitcast.160), kind=kOutput, calls=%fused_computation.43 | convolution fusion | flops 134479872 | bytes 3407872 | tf_op jit(solution)/shard_map/wkgtu,wtkgd->wukd/dot_general | solution.py:129
  113.6 1.6 gather_fusion.7
  115.4 10.0 %fusion.29 = f32[8192,256]{1,0:T(8,128)} fusion(bf16[512,128]{1,0:T(8,128)(2,1)S(1)} %get-tuple-element.31, bf16[512,128]{1,0:T(8,128)(2,1)S(1)} %get-tuple-element.30, bf16[512,8192]{1,0:T(8,128)(2,1)} %all-gather.2.cloned.1.call-done, f32[512]{0:T(512)S(1)} %add_rsqrt_fusion), kind=kOutput, calls=%fused_computation.50 | convolution fusion | flops 2160590848 | bytes 17041408 | tf_op jit(solution)/shard_map/dot_general | solution.py:155
  125.6 0.2 select_reduce_fusion.5
  125.8 0.6 dynamic_slice.26
  126.5 0.6 dynamic_slice.25
  127.1 0.6 dynamic_slice.29
  127.7 0.6 dynamic_slice.24
  131.0 0.6 dynamic_slice.27
  132.7 0.7 compare_select_fusion.13
  133.4 0.7 broadcast_compare_fusion.1
  134.1 0.7 compare_and_fusion
  134.7 3.5 %convert_bitcast_fusion = bf16[16,64,1,8,128]{4,1,3,0,2:T(8,128)(2,1)S(1)} fusion(bf16[16,64,128,1]{2,1,3,0:T(8,128)(2,1)S(1)} %bitcast.170, f32[16,8,64]{2,1,0:T(8,128)S(1)} %fusion.6, f32[16,8,64]{2,1,0:T(8,128)S(1)} %get-tuple-element.48, f32[16,64,64,8]{2,1,3,0:T(8,128)} %copy-done.2, pred[16,64,64]{1,2,0:T(8,128)(4,1)S(1)} %broadcast_and_fusion), kind=kOutput, calls=%fused_computation.35 | convolution fusion | flops 137887744 | bytes 4587520 | tf_op jit(solution)/shard_map/wkgtu,wukd->wtkgd/dot_general | solution.py:120
  138.3 1.8 copy.21
  140.1 2.0 copy.46
  142.0 4.6 %gather_fusion.4 = bf16[512,1024]{1,0:T(8,128)(2,1)S(1)} fusion(bf16[1024,1024]{1,0:T(8,128)(2,1)} %bitcast.158, s32[1024]{0:T(1024)S(1)} %pad_clamp_fusion.3), kind=kCustom, calls=%fused_computation.6 | custom fusion | bytes 2099200 | tf_op jit(solution)/shard_map/gather | solution.py:142
  146.7 0.1 broadcast_select_fusion
  146.8 1.0 copy-done.3
  147.9 0.9 gather_fusion.9
  148.7 0.8 broadcast_select_fusion.3
  149.5 4.1 %collective-permute-start = (bf16[128,1024]{1,0:T(8,128)(2,1)}, bf16[128,1024]{1,0:T(8,128)(2,1)}, u32[]{:S(2)}, u32[]{:S(2)}) collective-permute-start(bf16[128,1024]{1,0:T(8,128)(2,1)} %broadcast_select_fusion.3), channel_id=1, source_target_pairs={{0,4},{4,8},{8,12},{12,16},{16,20},{20,24},{24,28},{1,5},{5,9},{9,... | collective-permute-start | bytes 786440 | tf_op jit(solution)/shard_map/ppermute | solution.py:20
  153.6 0.9 gather_fusion.10
  154.6 1.3 collective-permute-start.1
  155.9 1.3 compare_and_fusion.2
  157.2 1.3 compare_select_fusion.9
  158.5 1.1 collective-permute-done
  159.5 5.2 %collective-permute-done.1 = bf16[128,1024]{1,0:T(8,128)(2,1)S(1)} collective-permute-done((bf16[128,1024]{1,0:T(8,128)(2,1)S(1)}, bf16[128,1024]{1,0:T(8,128)(2,1)S(1)}, u32[]{:S(2)}, u32[]{:S(2)}) %collective-permute-start.1) | collective-permute-done | bytes 262176 | tf_op jit(solution)/shard_map/ppermute | solution.py:20
  164.7 2.8 maximum_maximum_fusion
  167.4 3.2 %gather_fusion.5 = bf16[256,1024]{1,0:T(8,128)(2,1)S(1)} fusion(bf16[769,1024]{1,0:T(8,128)(2,1)} %maximum_maximum_fusion, s32[1024]{0:T(1024)S(1)} %pad_clamp_fusion), kind=kCustom, calls=%fused_computation.7 | custom fusion | bytes 1049600 | tf_op jit(solution)/shard_map/jit(_take)/gather | solution.py:203
  170.6 0.9 broadcast_select_fusion.1
  171.6 108.5 %reduce-scatter.2.cloned.1.call-done = f32[1024,256]{1,0:T(8,128)} async-done(((f32[8192,256]{1,0:T(8,128)}), f32[1024,256]{1,0:T(8,128)}) %reduce-scatter.2.cloned.1.call-update) | async-done | bytes 1048592 | tf_op jit(solution)/shard_map/reduce_scatter | solution.py:205
  280.1 2.2 fusion.59
  (48 shorter events, 2.1 us)
Async XLA Ops:
  7.2 68.7 %copy-start = (bf16[8192,128]{1,0:T(8,128)(2,1)S(1)}, bf16[8192,128]{1,0:T(8,128)(2,1)}, u32[]{:S(2)}) copy-start(bf16[8192,128]{1,0:T(8,128)(2,1)} %param.12) | copy-start | bytes 6291460
  7.2 63.4 %all-gather.2.cloned.1.call-start = ((), (), s32[]{:S(2)}) async-start(), calls=%async_computation.1 | async-start | bytes 10485760 | tf_op jit(solution)/shard_map/all_gather | solution.py:77
  7.9 272.2 %reduce-scatter.2.cloned.1.call-start = ((), (), s32[]{:S(2)}) async-start(), calls=%async_computation.2 | async-start | bytes 9437184 | tf_op jit(solution)/shard_map/reduce_scatter | solution.py:205
  11.9 6.9 %copy-start.1 = (bf16[512,1024]{1,0:T(8,128)(2,1)S(1)}, bf16[512,1024]{1,0:T(8,128)(2,1)}, u32[]{:S(2)}) copy-start(bf16[512,1024]{1,0:T(8,128)(2,1)} %param.10) | copy-start | bytes 3145732
  24.1 3.9 %copy-start.6 = (s32[8,8]{1,0:T(8,128)S(1)}, s32[8,8]{1,0:T(8,128)}, u32[]{:S(2)}) copy-start(s32[8,8]{1,0:T(8,128)} %param.14) | copy-start | bytes 772
  70.6 5.8 %copy-start.4 = (bf16[512,8192]{1,0:T(8,128)(2,1)S(1)}, bf16[512,8192]{1,0:T(8,128)(2,1)}, u32[]{:S(2)}) copy-start(bf16[512,8192]{1,0:T(8,128)(2,1)} %all-gather.2.cloned.1.call-done) | copy-start | bytes 25165828
  91.8 5.4 %copy-start.5 = (bf16[128,8,8,128]{3,2,1,0:T(8,128)(2,1)S(1)}, bf16[128,8,8,128]{3,2,1,0:T(8,128)(2,1)}, u32[]{:S(2)}) copy-start(bf16[128,8,8,128]{3,2,1,0:T(8,128)(2,1)} %copy.31) | copy-start | bytes 6291460
  95.7 6.2 %copy-start.2 = (f32[16,64,64,8]{2,1,3,0:T(8,128)}, f32[16,64,64,8]{2,1,3,0:T(8,128)S(1)}, u32[]{:S(2)}) copy-start(f32[16,64,64,8]{2,1,3,0:T(8,128)S(1)} %get-tuple-element.49) | copy-start | bytes 6291460
  146.8 1.0 copy-start.3
  149.5 10.0 %collective-permute-start = (bf16[128,1024]{1,0:T(8,128)(2,1)}, bf16[128,1024]{1,0:T(8,128)(2,1)}, u32[]{:S(2)}, u32[]{:S(2)}) collective-permute-start(bf16[128,1024]{1,0:T(8,128)(2,1)} %broadcast_select_fusion.3), channel_id=1, source_target_pairs={{0,4},{4,8},{8,12},{12,16},{16,20},{20,24},{24,28},{1,5},{5,9},{9,... | collective-permute-start | bytes 786440 | tf_op jit(solution)/shard_map/ppermute | solution.py:20
  154.6 10.1 %collective-permute-start.1 = (bf16[128,1024]{1,0:T(8,128)(2,1)S(1)}, bf16[128,1024]{1,0:T(8,128)(2,1)S(1)}, u32[]{:S(2)}, u32[]{:S(2)}) collective-permute-start(bf16[128,1024]{1,0:T(8,128)(2,1)S(1)} %broadcast_select_fusion.2), channel_id=1, source_target_pairs={{4,0},{8,4},{12,8},{16,12},{20,16},{24,20},{28,24},{5,1},{9,5},{13... | collective-permute-start | bytes 786440 | tf_op jit(solution)/shard_map/ppermute | solution.py:20
Sparse Core Ops, SparseCore 0:
  9.6 60.9 all-gather.1
  125.5 154.5 reduce-scatter.1
where the time goes:
time: 290 us; the launch traced here: 289 us
  waiting for transfers between devices  136 us (47%)
  local copies, waits for them, and re-layouts  61 us (21%)
  other arithmetic  35 us (12%)
  matrix products  33.9 us (12%)
  between operations  18.2 us (6%)
  starting transfers between devices  5.45 us (2%)
    reduce_scatter x1, waiting for transfers between devices, body(): lax.psum_scatter(make_term(normed, joined), 'dp', scatter_dimension=0, ti...  109 us
    all_gather x1, waiting for transfers between devices, layer_pass(): full_rows = lax.all_gather(hidden_rows, 'mp', axis=1, tiled=True)  20.1 us
    unnamed x17, local copies, waits for them, and re-layouts  10.9 us
    gather x3, other arithmetic, layer_pass(): row_offset = jnp.clip(positions - window_start[row_window], 0, LMAX - 1)  10.1 us
    dot_general x1, matrix products, make_term(): lax.dot_general(normed, cots, (((0,), (0,)), ((), ())), preferred_element...  10 us
    gather x2, local copies, waits for them, and re-layouts, layer_pass(): segments[index] == window_seg[:, None]  6.93 us
    dot_general x1, matrix products, layer_pass(): jnp.dot(normed, value_weight, preferred_element_type=jnp.float32)  6.36 us
    ppermute x2, waiting for transfers between devices, passed_along(): lax.ppermute(value, axis, [(source, source + steps) for source in range(f...  6.23 us
  transfers between devices with their start and end apart: 4, of which 4 were waited for; matrix products, arithmetic and copies ran while one was open for 25% of the time, Pallas kernels for 0%

commit v1 on v0

v1 whole, which is shorter than its diff:
```python
import jax
import jax.numpy as jnp
from jax import lax
from jax.experimental import pallas as pl
from jax.experimental.pallas import tpu as pltpu
from jax.sharding import PartitionSpec as P

HD = 128
CAP_R = 512
CAP_L = 256
PIECE = 128
LAST_START = CAP_R - PIECE

epsilon = 1e-06
masked_score = -1e30


def passed_along(value, axis, steps):
    count = lax.axis_size(axis)
    first, last = (max(0, -steps), min(count, count - steps))
    return lax.ppermute(value, axis, [(source, source + steps) for source in range(first, last)])


def derive_moves(lengths):
    device_total, slot_total = lengths.shape
    used_slots = jnp.sum((lengths > 0).astype(jnp.int32), axis=1)
    heavy_flag = used_slots >= 6
    devices = jnp.arange(device_total, dtype=jnp.int32)
    left_heavy = jnp.concatenate([jnp.zeros((1,), bool), heavy_flag[:-1]])
    light_left = ((devices > 0) & jnp.logical_not(left_heavy)).astype(jnp.int32)
    sent_left = jnp.where(heavy_flag, (used_slots - 4) // 2, light_left)
    kept_count = jnp.where(heavy_flag, 4, 1).astype(jnp.int32)
    slot_ids = jnp.arange(slot_total, dtype=jnp.int32)[None, :]
    return jnp.where(
        slot_ids < sent_left[:, None],
        -1,
        jnp.where(
            slot_ids < (sent_left + kept_count)[:, None],
            0,
            jnp.where(slot_ids < used_slots[:, None], 1, 0),
        ),
    )


def learner_rows(lengths, advantage, device):
    device_total, slot_total = lengths.shape
    moves = derive_moves(lengths)
    slot_ids = jnp.arange(slot_total, dtype=jnp.int32)
    before = (slot_ids[:, None] < slot_ids[None, :]).astype(jnp.int32)
    begins = jnp.sum(lengths[:, :, None] * before[None], axis=1)
    piece_start = jnp.minimum(jnp.sum(jnp.where(moves < 1, lengths, 0), axis=1), LAST_START)
    bases = jnp.stack(
        [begins - piece_start[:, None], begins + PIECE, begins + PIECE + CAP_R], axis=0
    )
    table = jnp.pad(lengths, ((1, 1), (0, 0)))
    window = lax.dynamic_slice_in_dim(table, device, 3, 0)
    move_window = lax.dynamic_slice_in_dim(jnp.pad(moves, ((1, 1), (0, 0))), device, 3, 0)
    rate_window = lax.dynamic_slice_in_dim(jnp.pad(advantage, ((1, 1), (0, 0))), device, 3, 0)
    base_window = lax.dynamic_slice_in_dim(jnp.pad(bases, ((0, 0), (1, 1), (0, 0))), device, 3, 1)
    base_window = jnp.stack([base_window[0, 0], base_window[1, 1], base_window[2, 2]], axis=0)
    wanted = jnp.array([1, 0, -1], jnp.int32)[:, None]
    sizes = jnp.where(move_window == wanted, window, 0).reshape(-1)
    rates = rate_window.reshape(-1) / jnp.maximum(sizes, 1).astype(jnp.float32)
    places = base_window.reshape(-1)
    ids = jnp.arange(3 * slot_total, dtype=jnp.int32)
    starts = jnp.sum(jnp.where(ids[:, None] < ids[None, :], sizes[:, None], 0), axis=0)
    ends = starts + sizes
    rows = jnp.arange(CAP_L, dtype=jnp.int32)
    hits = (rows[:, None] >= starts[None, :]) & (rows[:, None] < ends[None, :])
    segments = jnp.sum((rows[:, None] >= ends[None, :]).astype(jnp.int32), axis=1)
    scales = jnp.sum(jnp.where(hits, rates[None, :], 0.0), axis=1)
    source = jnp.sum(jnp.where(hits, (places - starts)[None, :] + rows[:, None] + 1, 0), axis=1) - 1
    own_piece = lax.dynamic_index_in_dim(piece_start, device, 0, keepdims=False)
    return segments, scales, source, own_piece


def attention_kernel(q_ref, k_ref, v_ref, u_ref, scale_ref, seg_col_ref, seg_row_ref,
                     out_ref, cots_ref, key_acc, value_acc):
    head = pl.program_id(0)
    inverse_root = HD ** (-0.5)
    rows = q_ref.shape[0]
    query, key, value = q_ref[...], k_ref[...], v_ref[...]
    cot = (scale_ref[...] * u_ref[...].astype(jnp.float32)).astype(jnp.bfloat16)
    t = lax.broadcasted_iota(jnp.int32, (rows, rows), 0)
    u = lax.broadcasted_iota(jnp.int32, (rows, rows), 1)
    allowed = (u <= t) & (seg_col_ref[...] == seg_row_ref[...])
    across = (((1,), (1,)), ((), ()))
    down = (((0,), (0,)), ((), ()))
    scores = lax.dot_general(query, key, across, preferred_element_type=jnp.float32) * inverse_root
    scores = jnp.where(allowed, scores, masked_score)
    raised = jnp.exp(scores - jnp.max(scores, axis=-1, keepdims=True))
    probability = raised * (1.0 / jnp.sum(raised, axis=-1, keepdims=True))
    weights = probability.astype(jnp.bfloat16)
    out_ref[...] = jnp.dot(weights, value, preferred_element_type=jnp.float32).astype(jnp.bfloat16)
    prob_grad = lax.dot_general(cot, value, across, preferred_element_type=jnp.float32)
    centre = jnp.sum(probability * prob_grad, axis=-1, keepdims=True)
    score_grad = (probability * (prob_grad - centre)).astype(jnp.bfloat16)
    key_term = lax.dot_general(score_grad, query, down, preferred_element_type=jnp.float32)
    value_term = lax.dot_general(weights, cot, down, preferred_element_type=jnp.float32)

    @pl.when(head == 0)
    def _():
        key_acc[...] = key_term
        value_acc[...] = value_term

    @pl.when(head > 0)
    def _():
        key_acc[...] += key_term
        value_acc[...] += value_term

    @pl.when(head == pl.num_programs(0) - 1)
    def _():
        cots_ref[:, :HD] = (key_acc[...] * inverse_root).astype(jnp.bfloat16)
        cots_ref[:, HD:] = value_acc[...].astype(jnp.bfloat16)


def attend(queries, keys_values, upstream, scales, segments):
    rows, width = queries.shape
    head_block = pl.BlockSpec((rows, HD), lambda h: (0, h))
    whole = lambda shape: pl.BlockSpec(shape, lambda h: (0, 0))
    return pl.pallas_call(
        attention_kernel,
        grid=(width // HD,),
        in_specs=[
            head_block,
            pl.BlockSpec((rows, HD), lambda h: (0, 0)),
            pl.BlockSpec((rows, HD), lambda h: (0, 1)),
            head_block,
            whole((rows, 1)),
            whole((rows, 1)),
            whole((1, rows)),
        ],
        out_specs=[head_block, whole((rows, 2 * HD))],
        out_shape=[
            jax.ShapeDtypeStruct((rows, width), jnp.bfloat16),
            jax.ShapeDtypeStruct((rows, 2 * HD), jnp.bfloat16),
        ],
        scratch_shapes=[pltpu.VMEM((rows, HD), jnp.float32), pltpu.VMEM((rows, HD), jnp.float32)],
        compiler_params=pltpu.CompilerParams(dimension_semantics=("arbitrary",)),
    )(queries, keys_values, keys_values, upstream, scales[:, None], segments[:, None], segments[None, :])


def body(hidden, queries, upstream, key_weight, value_weight, lengths, advantage):
    device = lax.axis_index("dp")
    segments, scales, source, own_piece = learner_rows(lengths, advantage, device)
    positions = jnp.arange(2 * PIECE + CAP_R, dtype=jnp.int32)
    pick = (source[:, None] == positions[None, :]).astype(jnp.bfloat16)

    def exchanged(array):
        later = lax.dynamic_slice_in_dim(array, own_piece, PIECE, 0)
        return passed_along(later, "dp", 1), passed_along(array[:PIECE], "dp", -1)

    def settled(array, pieces):
        pool = jnp.concatenate([pieces[0], array, pieces[1]], axis=0)
        return jnp.dot(pick, pool, preferred_element_type=jnp.float32).astype(jnp.bfloat16)

    hidden_pieces = exchanged(hidden)
    query_pieces = exchanged(queries)
    upstream_pieces = exchanged(upstream)
    full = lax.all_gather(settled(hidden, hidden_pieces), "mp", axis=1, tiled=True)
    query_rows = settled(queries, query_pieces)
    upstream_rows = settled(upstream, upstream_pieces)
    weight = jnp.concatenate([key_weight, value_weight], axis=1)
    widened = full.astype(jnp.float32)
    normed = (
        widened * lax.rsqrt(jnp.mean(widened * widened, axis=1, keepdims=True) + epsilon)
    ).astype(jnp.bfloat16)
    keys_values = jnp.dot(normed, weight, preferred_element_type=jnp.float32).astype(jnp.bfloat16)
    attention_out, cots = attend(query_rows, keys_values, upstream_rows, scales, segments)
    term = lax.dot_general(
        normed, cots, (((0,), (0,)), ((), ())), preferred_element_type=jnp.float32
    ).astype(jnp.bfloat16)
    summed = lax.psum_scatter(term, "dp", scatter_dimension=0, tiled=True).astype(jnp.float32)
    return (attention_out, summed[:, :HD], summed[:, HD:])


def solution(mesh):
    in_specs = (P("dp", "mp"), P("dp", "mp"), P("dp", "mp"), P(None, "mp"), P(None, "mp"), P(), P())
    out_specs = (P("dp", "mp"), P("dp", "mp"), P("dp", "mp"))
    return jax.shard_map(body, mesh=mesh, in_specs=in_specs, out_specs=out_specs, check_vma=False)
```

time: 290 us -> 201 us (0.69)
  local copies, waits for them, and re-layouts: 61 us -> 6.24 us
  other arithmetic: 35 us -> 6.96 us
  starting transfers between devices: 5.45 us -> 21.5 us
  matrix products: 33.9 us -> 18.4 us
  waiting for transfers between devices: 136 us -> 122 us
  Pallas kernels: 0 us -> 10.1 us
    gather x13 -> x0, local copies, waits for them, and re-layouts: 37.4 us -> none  [the longest x2 6.93 us: layer_pass(): segments[index] == window_seg[:, None]]
    ppermute x2 -> x6, waiting for transfers between devices: 6.23 us -> 28.2 us  [passed_along(): lax.ppermute(value, axis, [(source, source + steps) for source in range(f...]
    reduce_scatter x1, waiting for transfers between devices: 109 us -> 88.1 us  [body(): lax.psum_scatter(term, 'dp', scatter_dimension=0, tiled=True)]
    ppermute x2 -> x6, starting transfers between devices: 5.37 us -> 21.5 us  [passed_along(): lax.ppermute(value, axis, [(source, source + steps) for source in range(f...]
    dot_general x8 -> x5, matrix products: 33.9 us -> 18.4 us  [the longest x3 8.89 us: settled(): jnp.dot(pick, pool, preferred_element_type=jnp.float32).astype(jnp.bfloat16)]
    all_gather x1, waiting for transfers between devices: 20.1 us -> 5.2 us  [body(): lax.all_gather(settled(hidden, hidden_pieces), 'mp', axis=1, tiled=True)]
    unnamed x17 -> x12, local copies, waits for them, and re-layouts: 10.9 us -> 0.2 us
    pallas_call x0 -> x1, Pallas kernels: none -> 10.1 us  [attend(): pl.pallas_call(attention_kernel, grid=(width // HD,), in_specs=[head_bloc...]
  transfers between devices with their start and end apart: 4 -> 8, of which waited for: 4 -> 6; matrix products, arithmetic and copies ran while one was open for 25% -> 4% of each run, Pallas kernels for 0% -> 0%
where the time goes in v1:
time: 201 us
  waiting for transfers between devices  122 us (61%)
  starting transfers between devices  21.5 us (11%)
  matrix products  18.4 us (9%)
  between operations  16.1 us (8%)
  Pallas kernels  10.1 us (5%)
  other arithmetic  6.96 us (3%)
  local copies, waits for them, and re-layouts  6.24 us (3%)
    reduce_scatter x1, waiting for transfers between devices, body(): lax.psum_scatter(term, 'dp', scatter_dimension=0, tiled=True)  88.1 us
    ppermute x6, waiting for transfers between devices, passed_along(): lax.ppermute(value, axis, [(source, source + steps) for source in range(f...  28.2 us
    ppermute x6, starting transfers between devices, passed_along(): lax.ppermute(value, axis, [(source, source + steps) for source in range(f...  21.5 us
    pallas_call x1, Pallas kernels, attend(): pl.pallas_call(attention_kernel, grid=(width // HD,), in_specs=[head_bloc...  10.1 us
    dot_general x3, matrix products, settled(): jnp.dot(pick, pool, preferred_element_type=jnp.float32).astype(jnp.bfloat16)  8.89 us
    dot_general x1, matrix products, body(): lax.dot_general(normed, cots, (((0,), (0,)), ((), ())), preferred_element...  5.96 us
    all_gather x1, waiting for transfers between devices, body(): lax.all_gather(settled(hidden, hidden_pieces), 'mp', axis=1, tiled=True)  5.2 us
  transfers between devices with their start and end apart: 8, of which 6 were waited for; matrix products, arithmetic and copies ran while one was open for 4% of the time, Pallas kernels for 0%

profile of v1, /device:TPU:0, one launch (start us, length us, event | category | flops | bytes accessed | tf_op | source)
XLA Modules:
  0.0 200.9 jit_solution(8456020909057202301)
XLA Ops:
  7.2 0.0 all-gather.2.cloned.1.call-start
  7.2 0.8 convert_reduce_fusion.1
  8.0 0.1 select_add_fusion
  8.1 0.9 select_select_fusion
  9.0 0.6 dynamic_slice.28
  11.5 1.4 constant_dynamic-slice_fusion.1
  12.9 1.3 collective-permute-start.3
  14.2 6.3 %collective-permute-start.2 = (bf16[128,2048]{1,0:T(8,128)(2,1)S(1)}, bf16[128,2048]{1,0:T(8,128)(2,1)}, u32[]{:S(2)}, u32[]{:S(2)}) collective-permute-start(bf16[128,2048]{1,0:T(8,128)(2,1)S(1)} %get-tuple-element.11), channel_id=1, source_target_pairs={{0,4},{4,8},{8,12},{12,16},{16,20},{20,24},{24,28},{1,5},{5,9},{9,... | collective-permute-start | bytes 1572872 | tf_op jit(solution)/shard_map/ppermute | solution.py:21
  20.5 0.8 multiply_reduce_fusion
  21.3 0.1 bitcast_subtract_fusion
  21.4 0.8 fusion.46
  22.1 0.1 reshape.165
  22.2 0.1 broadcast_in_dim.87
  22.3 0.1 select_reduce_fusion.2
  22.4 0.1 convert_reduce_fusion
  22.5 0.0 copy-start.3
  22.5 0.0 copy-start.1
  22.5 0.0 copy-start.2
  22.5 7.2 %collective-permute-done.3 = bf16[128,2048]{1,0:T(8,128)(2,1)} collective-permute-done((bf16[128,2048]{1,0:T(8,128)(2,1)S(1)}, bf16[128,2048]{1,0:T(8,128)(2,1)}, u32[]{:S(2)}, u32[]{:S(2)}) %collective-permute-start.3) | collective-permute-done | bytes 524320 | tf_op jit(solution)/shard_map/ppermute | solution.py:21
  29.8 11.3 %collective-permute-done.2 = bf16[128,2048]{1,0:T(8,128)(2,1)} collective-permute-done((bf16[128,2048]{1,0:T(8,128)(2,1)S(1)}, bf16[128,2048]{1,0:T(8,128)(2,1)}, u32[]{:S(2)}, u32[]{:S(2)}) %collective-permute-start.2) | collective-permute-done | bytes 524320 | tf_op jit(solution)/shard_map/ppermute | solution.py:21
  41.1 3.8 %fusion.12 = bf16[256,2048]{1,0:T(8,128)(2,1)} fusion(bf16[128,2048]{1,0:T(8,128)(2,1)} %collective-permute-done.3, bf16[512,2048]{1,0:T(8,128)(2,1)} %param.8, bf16[128,2048]{1,0:T(8,128)(2,1)} %collective-permute-done.2, s32[256]{0:T(256)S(1)} %broadcast_add_fusion), kind=kOutput, calls=%fused_computation.15 | convolution fusion | flops 815464448 | bytes 4195328 | tf_op jit(solution)/shard_map/dot_general | solution.py:155
  44.9 0.0 copy-start.4
  44.9 0.0 all-gather.2.cloned.1.call-update
  44.9 0.0 reduce-scatter.2.cloned.1.call-start
  45.0 0.0 copy-done.1
  45.0 0.1 constant_dynamic-slice_fusion.2
  45.1 1.3 collective-permute-start.1
  46.4 5.9 %collective-permute-start = (bf16[128,1024]{1,0:T(8,128)(2,1)S(1)}, bf16[128,1024]{1,0:T(8,128)(2,1)}, u32[]{:S(2)}, u32[]{:S(2)}) collective-permute-start(bf16[128,1024]{1,0:T(8,128)(2,1)S(1)} %get-tuple-element.15), channel_id=1, source_target_pairs={{0,4},{4,8},{8,12},{12,16},{16,20},{20,24},{24,28},{1,5},{5,9},{9,... | collective-permute-start | bytes 786440 | tf_op jit(solution)/shard_map/ppermute | solution.py:21
  52.2 0.0 copy-done.2
  52.2 0.1 constant_dynamic-slice_fusion
  52.3 1.3 collective-permute-start.5
  53.6 5.4 %collective-permute-start.4 = (bf16[128,1024]{1,0:T(8,128)(2,1)S(1)}, bf16[128,1024]{1,0:T(8,128)(2,1)}, u32[]{:S(2)}, u32[]{:S(2)}) collective-permute-start(bf16[128,1024]{1,0:T(8,128)(2,1)S(1)} %get-tuple-element.13), channel_id=1, source_target_pairs={{0,4},{4,8},{8,12},{12,16},{16,20},{20,24},{24,28},{1,5},{5,9},{9,... | collective-permute-start | bytes 786440 | tf_op jit(solution)/shard_map/ppermute | solution.py:21
  59.1 0.0 copy-done.4
  59.1 0.1 reshape.166
  59.2 0.1 select_reduce_fusion
  59.3 0.8 copy.13.scale_ref
  60.1 0.0 copy-done.3
  60.1 0.8 copy.14.seg_col_ref
  60.9 0.0 collective-permute-done.1
  60.9 6.6 %collective-permute-done = bf16[128,1024]{1,0:T(8,128)(2,1)} collective-permute-done((bf16[128,1024]{1,0:T(8,128)(2,1)S(1)}, bf16[128,1024]{1,0:T(8,128)(2,1)}, u32[]{:S(2)}, u32[]{:S(2)}) %collective-permute-start) | collective-permute-done | bytes 262176 | tf_op jit(solution)/shard_map/ppermute | solution.py:21
  67.5 2.5 %fusion.32.q_ref = bf16[256,1024]{1,0:T(8,128)(2,1)} fusion(bf16[128,1024]{1,0:T(8,128)(2,1)} %collective-permute-done.1, bf16[512,1024]{1,0:T(8,128)(2,1)S(1)} %copy-done.1, bf16[128,1024]{1,0:T(8,128)(2,1)} %collective-permute-done, s32[256]{0:T(256)S(1)} %broadcast_add_fusion), kind=kOutput, calls=%fused_computation.29 | convolution fusion | flops 407830528 | bytes 2098176 | tf_op jit(solution)/shard_map/dot_general | solution.py:155
  70.0 0.0 collective-permute-done.5
  70.0 3.1 %collective-permute-done.4 = bf16[128,1024]{1,0:T(8,128)(2,1)} collective-permute-done((bf16[128,1024]{1,0:T(8,128)(2,1)S(1)}, bf16[128,1024]{1,0:T(8,128)(2,1)}, u32[]{:S(2)}, u32[]{:S(2)}) %collective-permute-start.4) | collective-permute-done | bytes 262176 | tf_op jit(solution)/shard_map/ppermute | solution.py:21
  73.0 0.0 copy-start.5
  73.0 2.6 %fusion.29.u_ref = bf16[256,1024]{1,0:T(8,128)(2,1)} fusion(bf16[128,1024]{1,0:T(8,128)(2,1)} %collective-permute-done.5, bf16[512,1024]{1,0:T(8,128)(2,1)S(1)} %copy-done.2, bf16[128,1024]{1,0:T(8,128)(2,1)} %collective-permute-done.4, s32[256]{0:T(256)S(1)} %broadcast_add_fusion), kind=kOutput, calls=%fused_computation.28 | convolution fusion | flops 407830528 | bytes 2098176 | tf_op jit(solution)/shard_map/dot_general | solution.py:155
  75.6 5.2 %all-gather.2.cloned.1.call-done = bf16[256,8192]{1,0:T(8,128)(2,1)} async-done(((bf16[256,2048]{1,0:T(8,128)(2,1)}), bf16[256,8192]{1,0:T(8,128)(2,1)}) %all-gather.2.cloned.1.call-update) | async-done | bytes 4194320 | tf_op jit(solution)/shard_map/all_gather | solution.py:160
  80.8 0.0 copy-start
  80.9 3.3 %fusion = f32[256]{0:T(256)S(1)} fusion(bf16[256,8192]{1,0:T(8,128)(2,1)} %all-gather.2.cloned.1.call-done), kind=kLoop, calls=%fused_computation.3 | loop fusion | flops 6291200 | bytes 4195328 | tf_op jit(solution)/shard_map/reduce_sum | solution.py:166
  84.1 0.0 copy-done.5
  84.1 0.2 copy-done
  84.3 3.6 %fusion.35.k_ref.v_ref = bf16[256,256]{1,0:T(8,128)(2,1)} fusion(bf16[8192,128]{1,0:T(8,128)(2,1)S(1)} %copy-done.5, bf16[8192,128]{1,0:T(8,128)(2,1)} %param.11, bf16[256,8192]{1,0:T(8,128)(2,1)S(1)} %copy-done, f32[256]{0:T(256)S(1)} %add_rsqrt_fusion), kind=kOutput, calls=%fused_computation.30 | convolution fusion | flops 1088487424 | bytes 8520704 | tf_op jit(solution)/shard_map/dot_general | solution.py:168
  87.9 10.1 %shard_map.103 = (bf16[256,1024]{1,0:T(8,128)(2,1)}, bf16[256,256]{1,0:T(8,128)(2,1)}) custom-call(bf16[256,1024]{1,0:T(8,128)(2,1)} %fusion.32.q_ref, bf16[256,256]{1,0:T(8,128)(2,1)} %fusion.35.k_ref.v_ref, bf16[256,256]{1,0:T(8,128)(2,1)} %fusion.35.k_ref.v_ref, bf16[256,1024]{1,0:T(8,128)(2,1)} %fusion.29.u_ref, f32[256,1]{1,0:T(8,128)} %copy.13.scale_ref, ...), custom_call_target="tpu_custom_call" | custom-call | tf_op jit(solution)/shard_map/pallas_call | solution.py:121
  98.0 6.0 %convolution_convert_fusion = bf16[8192,256]{1,0:T(8,128)(2,1)} fusion(bf16[256,256]{1,0:T(8,128)(2,1)} %get-tuple-element.6, bf16[256,8192]{1,0:T(8,128)(2,1)} %all-gather.2.cloned.1.call-done, f32[256]{0:T(256)S(1)} %add_rsqrt_fusion), kind=kOutput, calls=%fused_computation.2 | convolution fusion | flops 1082130432 | bytes 8520704 | tf_op jit(solution)/shard_map/dot_general | solution.py:170
  103.9 0.0 reduce-scatter.2.cloned.1.call-update
  104.0 88.1 %reduce-scatter.2.cloned.1.call-done = bf16[1024,256]{1,0:T(8,128)(2,1)} async-done(((bf16[8192,256]{1,0:T(8,128)(2,1)}), bf16[1024,256]{1,0:T(8,128)(2,1)}) %reduce-scatter.2.cloned.1.call-update) | async-done | bytes 524304 | tf_op jit(solution)/shard_map/reduce_scatter | solution.py:173
  192.0 2.1 %fusion.58 = (f32[1024,128]{1,0:T(8,128)}, f32[1024,128]{1,0:T(8,128)}) fusion(bf16[1024,256]{1,0:T(8,128)(2,1)} %reduce-scatter.2.cloned.1.call-done), kind=kLoop, calls=%fused_computation.90 | loop fusion | bytes 2097152 | tf_op jit(solution)/shard_map/slice | solution.py:174
  (10 shorter events, 0.1 us)
Async XLA Ops:
  7.2 73.7 %all-gather.2.cloned.1.call-start = ((), (), s32[]{:S(2)}) async-start(), calls=%async_computation.1 | async-start | bytes 5242880 | tf_op jit(solution)/shard_map/all_gather | solution.py:160
  12.9 16.9 %collective-permute-start.3 = (bf16[128,2048]{1,0:T(8,128)(2,1)S(1)}, bf16[128,2048]{1,0:T(8,128)(2,1)}, u32[]{:S(2)}, u32[]{:S(2)}) collective-permute-start(bf16[128,2048]{1,0:T(8,128)(2,1)S(1)} %get-tuple-element.12), channel_id=1, source_target_pairs={{4,0},{8,4},{12,8},{16,12},{20,16},{24,20},{28,24},{5,1},{9,5},{13... | collective-permute-start | bytes 1572872 | tf_op jit(solution)/shard_map/ppermute | solution.py:21
  14.2 26.9 %collective-permute-start.2 = (bf16[128,2048]{1,0:T(8,128)(2,1)S(1)}, bf16[128,2048]{1,0:T(8,128)(2,1)}, u32[]{:S(2)}, u32[]{:S(2)}) collective-permute-start(bf16[128,2048]{1,0:T(8,128)(2,1)S(1)} %get-tuple-element.11), channel_id=1, source_target_pairs={{0,4},{4,8},{8,12},{12,16},{16,20},{20,24},{24,28},{1,5},{5,9},{9,... | collective-permute-start | bytes 1572872 | tf_op jit(solution)/shard_map/ppermute | solution.py:21
  22.5 37.6 %copy-start.3 = (s32[256]{0:T(256)}, s32[256]{0:T(256)S(1)}, u32[]{:S(2)}) copy-start(s32[256]{0:T(256)S(1)} %get-tuple-element.7) | copy-start | bytes 3076
  22.5 22.5 %copy-start.1 = (bf16[512,1024]{1,0:T(8,128)(2,1)S(1)}, bf16[512,1024]{1,0:T(8,128)(2,1)}, u32[]{:S(2)}) copy-start(bf16[512,1024]{1,0:T(8,128)(2,1)} %param.9) | copy-start | bytes 3145732
  22.5 29.7 %copy-start.2 = (bf16[512,1024]{1,0:T(8,128)(2,1)S(1)}, bf16[512,1024]{1,0:T(8,128)(2,1)}, u32[]{:S(2)}) copy-start(bf16[512,1024]{1,0:T(8,128)(2,1)} %param.10) | copy-start | bytes 3145732
  44.9 14.2 %copy-start.4 = (f32[8,8]{1,0:T(8,128)S(1)}, f32[8,8]{1,0:T(8,128)}, u32[]{:S(2)}) copy-start(f32[8,8]{1,0:T(8,128)} %param.14) | copy-start | bytes 772
  44.9 147.1 %reduce-scatter.2.cloned.1.call-start = ((), (), s32[]{:S(2)}) async-start(), calls=%async_computation.2 | async-start | bytes 4718592 | tf_op jit(solution)/shard_map/reduce_scatter | solution.py:173
  45.1 15.8 %collective-permute-start.1 = (bf16[128,1024]{1,0:T(8,128)(2,1)S(1)}, bf16[128,1024]{1,0:T(8,128)(2,1)}, u32[]{:S(2)}, u32[]{:S(2)}) collective-permute-start(bf16[128,1024]{1,0:T(8,128)(2,1)S(1)} %get-tuple-element.16), channel_id=1, source_target_pairs={{4,0},{8,4},{12,8},{16,12},{20,16},{24,20},{28,24},{5,1},{9,5},{13... | collective-permute-start | bytes 786440 | tf_op jit(solution)/shard_map/ppermute | solution.py:21
  46.4 21.1 %collective-permute-start = (bf16[128,1024]{1,0:T(8,128)(2,1)S(1)}, bf16[128,1024]{1,0:T(8,128)(2,1)}, u32[]{:S(2)}, u32[]{:S(2)}) collective-permute-start(bf16[128,1024]{1,0:T(8,128)(2,1)S(1)} %get-tuple-element.15), channel_id=1, source_target_pairs={{0,4},{4,8},{8,12},{12,16},{16,20},{20,24},{24,28},{1,5},{5,9},{9,... | collective-permute-start | bytes 786440 | tf_op jit(solution)/shard_map/ppermute | solution.py:21
  52.3 17.7 %collective-permute-start.5 = (bf16[128,1024]{1,0:T(8,128)(2,1)S(1)}, bf16[128,1024]{1,0:T(8,128)(2,1)}, u32[]{:S(2)}, u32[]{:S(2)}) collective-permute-start(bf16[128,1024]{1,0:T(8,128)(2,1)S(1)} %get-tuple-element.14), channel_id=1, source_target_pairs={{4,0},{8,4},{12,8},{16,12},{20,16},{24,20},{28,24},{5,1},{9,5},{13... | collective-permute-start | bytes 786440 | tf_op jit(solution)/shard_map/ppermute | solution.py:21
  53.6 19.4 %collective-permute-start.4 = (bf16[128,1024]{1,0:T(8,128)(2,1)S(1)}, bf16[128,1024]{1,0:T(8,128)(2,1)}, u32[]{:S(2)}, u32[]{:S(2)}) collective-permute-start(bf16[128,1024]{1,0:T(8,128)(2,1)S(1)} %get-tuple-element.13), channel_id=1, source_target_pairs={{0,4},{4,8},{8,12},{12,16},{16,20},{20,24},{24,28},{1,5},{5,9},{9,... | collective-permute-start | bytes 786440 | tf_op jit(solution)/shard_map/ppermute | solution.py:21
  73.0 11.1 %copy-start.5 = (bf16[8192,128]{1,0:T(8,128)(2,1)S(1)}, bf16[8192,128]{1,0:T(8,128)(2,1)}, u32[]{:S(2)}) copy-start(bf16[8192,128]{1,0:T(8,128)(2,1)} %param.12) | copy-start | bytes 6291460
  80.8 3.4 %copy-start = (bf16[256,8192]{1,0:T(8,128)(2,1)S(1)}, bf16[256,8192]{1,0:T(8,128)(2,1)}, u32[]{:S(2)}) copy-start(bf16[256,8192]{1,0:T(8,128)(2,1)} %all-gather.2.cloned.1.call-done) | copy-start | bytes 12582916
Sparse Core Ops, SparseCore 0:
  45.0 35.7 all-gather.1
  104.1 87.8 reduce-scatter.1

commit v2 on v1

--- a/solution.py
+++ b/solution.py
@@ -1,3 +1,5 @@
+import functools
+
 import jax
 import jax.numpy as jnp
 from jax import lax
@@ -95,8 +97,8 @@
     prob_grad = lax.dot_general(cot, value, across, preferred_element_type=jnp.float32)
     centre = jnp.sum(probability * prob_grad, axis=-1, keepdims=True)
     score_grad = (probability * (prob_grad - centre)).astype(jnp.bfloat16)
-    key_term = lax.dot_general(score_grad, query, down, preferred_element_type=jnp.float32)
-    value_term = lax.dot_general(weights, cot, down, preferred_element_type=jnp.float32)
+    key_term = lax.dot_general(query, score_grad, down, preferred_element_type=jnp.float32)
+    value_term = lax.dot_general(cot, weights, down, preferred_element_type=jnp.float32)
 
     @pl.when(head == 0)
     def _():
@@ -110,8 +112,8 @@
 
     @pl.when(head == pl.num_programs(0) - 1)
     def _():
-        cots_ref[:, :HD] = (key_acc[...] * inverse_root).astype(jnp.bfloat16)
-        cots_ref[:, HD:] = value_acc[...].astype(jnp.bfloat16)
+        cots_ref[:HD] = (key_acc[...] * inverse_root).astype(jnp.bfloat16)
+        cots_ref[HD:] = value_acc[...].astype(jnp.bfloat16)
 
 
 def attend(queries, keys_values, upstream, scales, segments):
@@ -130,14 +132,113 @@
             whole((rows, 1)),
             whole((1, rows)),
         ],
-        out_specs=[head_block, whole((rows, 2 * HD))],
+        out_specs=[head_block, whole((2 * HD, rows))],
         out_shape=[
             jax.ShapeDtypeStruct((rows, width), jnp.bfloat16),
-            jax.ShapeDtypeStruct((rows, 2 * HD), jnp.bfloat16),
+            jax.ShapeDtypeStruct((2 * HD, rows), jnp.bfloat16),
         ],
-        scratch_shapes=[pltpu.VMEM((rows, HD), jnp.float32), pltpu.VMEM((rows, HD), jnp.float32)],
+        scratch_shapes=[pltpu.VMEM((HD, rows), jnp.float32), pltpu.VMEM((HD, rows), jnp.float32)],
         compiler_params=pltpu.CompilerParams(dimension_semantics=("arbitrary",)),
     )(queries, keys_values, keys_values, upstream, scales[:, None], segments[:, None], segments[None, :])
+
+
+def gradient_kernel(count, normed_ref, cots_ref, key_ref, value_ref, pair_out, pair_in, line_out,
+                    line_in, acc, pair_sent, pair_got, line_sent, line_got):
+    me = lax.axis_index("dp")
+    lines = count // 2
+    line, side = me // 2, me % 2
+    width = acc.shape[1]
+    mesh_id = pl.DeviceIdType.MESH
+
+    def place(k):
+        return (line + 1 + k) % lines
+
+    def share(owner):
+        columns = pl.ds(pl.multiple_of(owner * width, width), width)
+        return jnp.dot(cots_ref[...], normed_ref[:, columns], preferred_element_type=jnp.float32)
+
+    def pair_copy(k):
+        return pltpu.make_async_remote_copy(
+            src_ref=pair_out.at[k], dst_ref=pair_in.at[k],
+            send_sem=pair_sent.at[k], recv_sem=pair_got.at[k],
+            device_id={"dp": line * 2 + 1 - side}, device_id_type=mesh_id,
+        )
+
+    def line_copy(k):
+        return pltpu.make_async_remote_copy(
+            src_ref=line_out.at[k], dst_ref=line_in.at[k],
+            send_sem=line_sent.at[k], recv_sem=line_got.at[k],
+            device_id={"dp": place(k) * 2 + side}, device_id_type=mesh_id,
+        )
+
+    barrier = pltpu.get_barrier_semaphore()
+    pl.semaphore_signal(barrier, inc=1, device_id={"dp": line * 2 + 1 - side}, device_id_type=mesh_id)
+
+    @pl.loop(0, lines - 1)
+    def _(k):
+        pl.semaphore_signal(barrier, inc=1, device_id={"dp": place(k) * 2 + side}, device_id_type=mesh_id)
+
+    pl.semaphore_wait(barrier, lines)
+
+    @pl.loop(0, lines)
+    def _(k):
+        pair_out[k] = share(place(k) * 2 + 1 - side).astype(jnp.bfloat16)
+        pair_copy(k).start()
+
+    @pl.loop(0, lines - 1)
+    def _(k):
+        own = share(place(k) * 2 + side)
+        pair_copy(k).wait_recv()
+        line_out[k] = (own + pair_in[k].astype(jnp.float32)).astype(jnp.bfloat16)
+        line_copy(k).start()
+
+    acc[...] = share(me)
+    pair_copy(lines - 1).wait_recv()
+    acc[...] += pair_in[lines - 1].astype(jnp.float32)
+
+    @pl.loop(0, lines - 1)
+    def _(k):
+        line_copy(k).wait_recv()
+        acc[...] += line_in[k].astype(jnp.float32)
+
+    key_ref[...] = acc[:HD].T
+    value_ref[...] = acc[HD:].T
+
+    @pl.loop(0, lines)
+    def _(k):
+        pair_copy(k).wait_send()
+
+    @pl.loop(0, lines - 1)
+    def _(k):
+        line_copy(k).wait_send()
+
+
+def gradient_sum(normed, cots):
+    count = lax.axis_size("dp")
+    lines = count // 2
+    width = normed.shape[1] // count
+    vmem = pl.BlockSpec(memory_space=pltpu.VMEM)
+    shares = lambda n: pltpu.VMEM((n, 2 * HD, width), jnp.bfloat16)
+    return pl.pallas_call(
+        functools.partial(gradient_kernel, count),
+        in_specs=[vmem, vmem],
+        out_specs=[vmem, vmem],
+        out_shape=[jax.ShapeDtypeStruct((width, HD), jnp.float32)] * 2,
+        scratch_shapes=[
+            shares(lines),
+            shares(lines),
+            shares(lines - 1),
+            shares(lines - 1),
+            pltpu.VMEM((2 * HD, width), jnp.float32),
+            pltpu.SemaphoreType.DMA((lines,)),
+            pltpu.SemaphoreType.DMA((lines,)),
+            pltpu.SemaphoreType.DMA((lines - 1,)),
+            pltpu.SemaphoreType.DMA((lines - 1,)),
+        ],
+        compiler_params=pltpu.CompilerParams(
+            collective_id=0, has_side_effects=True, vmem_limit_bytes=40 * 1024 * 1024
+        ),
+    )(normed, cots)
 
 
 def body(hidden, queries, upstream, key_weight, value_weight, lengths, advantage):
@@ -167,11 +268,8 @@
     ).astype(jnp.bfloat16)
     keys_values = jnp.dot(normed, weight, preferred_element_type=jnp.float32).astype(jnp.bfloat16)
     attention_out, cots = attend(query_rows, keys_values, upstream_rows, scales, segments)
-    term = lax.dot_general(
-        normed, cots, (((0,), (0,)), ((), ())), preferred_element_type=jnp.float32
-    ).astype(jnp.bfloat16)
-    summed = lax.psum_scatter(term, "dp", scatter_dimension=0, tiled=True).astype(jnp.float32)
-    return (attention_out, summed[:, :HD], summed[:, HD:])
+    key_grad, value_grad = gradient_sum(normed, cots)
+    return (attention_out, key_grad, value_grad)
 
 
 def solution(mesh):

time: 201 us -> 174 us (0.87)
  waiting for transfers between devices: 122 us -> 35.6 us
  Pallas kernels: 10.1 us -> 73.2 us
  matrix products: 18.4 us -> 10.6 us
  local copies, waits for them, and re-layouts: 6.24 us -> 9.95 us
    reduce_scatter x1 -> x0, waiting for transfers between devices: 88.1 us -> none  [body(): lax.psum_scatter(term, 'dp', scatter_dimension=0, tiled=True)]
    pallas_call x0 -> x1, Pallas kernels: none -> 63.7 us  [gradient_sum(): pl.pallas_call(functools.partial(gradient_kernel, count), in_specs=[vmem,...]
    dot_general x1 -> x0, matrix products: 5.96 us -> none  [body(): lax.dot_general(normed, cots, (((0,), (0,)), ((), ())), preferred_element...]
    unnamed x12 -> x22, local copies, waits for them, and re-layouts: 0.2 us -> 5.98 us
    all_gather x1, waiting for transfers between devices: 5.2 us -> 7.92 us  [body(): lax.all_gather(settled(hidden, hidden_pieces), 'mp', axis=1, tiled=True)]
    slice x1 -> x0, local copies, waits for them, and re-layouts: 2.06 us -> none  [body(): return (attention_out, summed[:, :HD], summed[:, HD:])]
  transfers between devices with their start and end apart: 8 -> 7, of which waited for: 6 -> 4; matrix products, arithmetic and copies ran while one was open for 4% -> 5% of each run, Pallas kernels for 0% -> 0%
where the time goes in v2:
time: 174 us; the launch traced here: 173 us
  Pallas kernels  73.2 us (42%)
  waiting for transfers between devices  35.6 us (20%)
  starting transfers between devices  19.7 us (11%)
  between operations  16.2 us (9%)
  matrix products  10.6 us (6%)
  local copies, waits for them, and re-layouts  9.95 us (6%)
  other arithmetic  8.08 us (5%)
    pallas_call x1, Pallas kernels, gradient_sum(): pl.pallas_call(functools.partial(gradient_kernel, count), in_specs=[vmem,...  63.7 us
    ppermute x6, waiting for transfers between devices, passed_along(): lax.ppermute(value, axis, [(source, source + steps) for source in range(f...  27.6 us
    ppermute x6, starting transfers between devices, passed_along(): lax.ppermute(value, axis, [(source, source + steps) for source in range(f...  19.7 us
    pallas_call x1, Pallas kernels, attend(): pl.pallas_call(attention_kernel, grid=(width // HD,), in_specs=[head_bloc...  9.49 us
    dot_general x3, matrix products, settled(): jnp.dot(pick, pool, preferred_element_type=jnp.float32).astype(jnp.bfloat16)  8.64 us
    all_gather x1, waiting for transfers between devices, body(): lax.all_gather(settled(hidden, hidden_pieces), 'mp', axis=1, tiled=True)  7.92 us
    unnamed x22, local copies, waits for them, and re-layouts  5.98 us
  transfers between devices with their start and end apart: 7, of which 4 were waited for; matrix products, arithmetic and copies ran while one was open for 5% of the time, Pallas kernels for 0%

profile of v2, /device:TPU:0, one launch (start us, length us, event | category | flops | bytes accessed | tf_op | source)
XLA Modules:
  0.0 173.3 jit_solution(14067690140234620248)
XLA Ops:
  7.2 0.0 all-gather.2.cloned.1.call-start
  7.2 0.8 convert_reduce_fusion.1
  8.0 0.1 select_add_fusion
  8.1 0.9 select_select_fusion
  9.0 0.6 dynamic_slice.28
  11.5 1.4 constant_dynamic-slice_fusion.1
  12.9 5.7 %collective-permute-start.2 = (bf16[128,2048]{1,0:T(8,128)(2,1)S(1)}, bf16[128,2048]{1,0:T(8,128)(2,1)}, u32[]{:S(2)}, u32[]{:S(2)}) collective-permute-start(bf16[128,2048]{1,0:T(8,128)(2,1)S(1)} %get-tuple-element.15), channel_id=1, source_target_pairs={{0,4},{4,8},{8,12},{12,16},{16,20},{20,24},{24,28},{1,5},{5,9},{9,... | collective-permute-start | bytes 1572872 | tf_op jit(solution)/shard_map/ppermute | solution.py:23
  18.6 1.3 collective-permute-start.3
  19.9 0.8 multiply_reduce_fusion
  20.6 0.1 bitcast_subtract_fusion
  20.7 0.8 fusion.42
  21.5 0.1 broadcast_in_dim.87
  21.6 0.1 select_reduce_fusion.2
  21.7 0.1 reshape.165
  21.8 0.1 convert_reduce_fusion
  21.9 0.0 copy-start.6
  21.9 0.0 copy-start.4
  21.9 0.0 copy-start.5
  21.9 18.2 %collective-permute-done.2 = bf16[128,2048]{1,0:T(8,128)(2,1)} collective-permute-done((bf16[128,2048]{1,0:T(8,128)(2,1)S(1)}, bf16[128,2048]{1,0:T(8,128)(2,1)}, u32[]{:S(2)}, u32[]{:S(2)}) %collective-permute-start.2) | collective-permute-done | bytes 524320 | tf_op jit(solution)/shard_map/ppermute | solution.py:23
  40.2 0.0 collective-permute-done.3
  40.2 3.8 %fusion.12 = bf16[256,2048]{1,0:T(8,128)(2,1)} fusion(bf16[128,2048]{1,0:T(8,128)(2,1)} %collective-permute-done.3, bf16[512,2048]{1,0:T(8,128)(2,1)} %param.8, bf16[128,2048]{1,0:T(8,128)(2,1)} %collective-permute-done.2, s32[256]{0:T(256)S(1)} %broadcast_add_fusion), kind=kOutput, calls=%fused_computation.14 | convolution fusion | flops 815464448 | bytes 4195328 | tf_op jit(solution)/shard_map/dot_general | solution.py:256
  44.0 0.0 copy-start.7
  44.0 0.0 all-gather.2.cloned.1.call-update
  44.0 0.0 copy-done.4
  44.0 0.1 constant_dynamic-slice_fusion
  44.1 4.5 %collective-permute-start.4 = (bf16[128,1024]{1,0:T(8,128)(2,1)S(1)}, bf16[128,1024]{1,0:T(8,128)(2,1)S(1)}, u32[]{:S(2)}, u32[]{:S(2)}) collective-permute-start(bf16[128,1024]{1,0:T(8,128)(2,1)S(1)} %get-tuple-element.17), channel_id=1, source_target_pairs={{0,4},{4,8},{8,12},{12,16},{16,20},{20,24},{24,28},{1,5},{5,9},{9,... | collective-permute-start | bytes 786440 | tf_op jit(solution)/shard_map/ppermute | solution.py:23
  48.6 1.3 collective-permute-start.5
  49.9 0.0 copy-done.5
  49.9 0.1 constant_dynamic-slice_fusion.2
  50.0 5.6 %collective-permute-start = (bf16[128,1024]{1,0:T(8,128)(2,1)S(1)}, bf16[128,1024]{1,0:T(8,128)(2,1)}, u32[]{:S(2)}, u32[]{:S(2)}) collective-permute-start(bf16[128,1024]{1,0:T(8,128)(2,1)S(1)} %get-tuple-element.19), channel_id=1, source_target_pairs={{0,4},{4,8},{8,12},{12,16},{16,20},{20,24},{24,28},{1,5},{5,9},{9,... | collective-permute-start | bytes 786440 | tf_op jit(solution)/shard_map/ppermute | solution.py:23
  55.7 1.3 collective-permute-start.1
  56.9 0.0 copy-done.7
  57.0 0.1 reshape.166
  57.1 0.1 select_reduce_fusion
  57.2 0.8 copy.13.scale_ref
  58.0 0.0 copy-done.6
  58.0 0.8 copy.14.seg_col_ref
  58.8 0.0 collective-permute-done.4
  58.8 0.5 collective-permute-done.5
  59.2 2.4 %fusion.27.u_ref = bf16[256,1024]{1,0:T(8,128)(2,1)} fusion(bf16[128,1024]{1,0:T(8,128)(2,1)} %collective-permute-done.5, bf16[512,1024]{1,0:T(8,128)(2,1)S(1)} %copy-done.4, bf16[128,1024]{1,0:T(8,128)(2,1)S(1)} %collective-permute-done.4, s32[256]{0:T(256)S(1)} %broadcast_add_fusion), kind=kOutput, calls=%fused_computation.27 | convolution fusion | flops 407830528 | bytes 2098176 | tf_op jit(solution)/shard_map/dot_general | solution.py:256
  61.6 8.9 %collective-permute-done = bf16[128,1024]{1,0:T(8,128)(2,1)} collective-permute-done((bf16[128,1024]{1,0:T(8,128)(2,1)S(1)}, bf16[128,1024]{1,0:T(8,128)(2,1)}, u32[]{:S(2)}, u32[]{:S(2)}) %collective-permute-start) | collective-permute-done | bytes 262176 | tf_op jit(solution)/shard_map/ppermute | solution.py:23
  70.5 0.0 collective-permute-done.1
  70.5 2.4 %fusion.30.q_ref = bf16[256,1024]{1,0:T(8,128)(2,1)} fusion(bf16[128,1024]{1,0:T(8,128)(2,1)} %collective-permute-done.1, bf16[512,1024]{1,0:T(8,128)(2,1)S(1)} %copy-done.5, bf16[128,1024]{1,0:T(8,128)(2,1)} %collective-permute-done, s32[256]{0:T(256)S(1)} %broadcast_add_fusion), kind=kOutput, calls=%fused_computation.28 | convolution fusion | flops 407830528 | bytes 2098176 | tf_op jit(solution)/shard_map/dot_general | solution.py:256
  73.0 7.9 %all-gather.2.cloned.1.call-done = bf16[256,8192]{1,0:T(8,128)(2,1)} async-done(((bf16[256,2048]{1,0:T(8,128)(2,1)}), bf16[256,8192]{1,0:T(8,128)(2,1)}) %all-gather.2.cloned.1.call-update) | async-done | bytes 4194320 | tf_op jit(solution)/shard_map/all_gather | solution.py:261
  80.9 0.0 copy-start.3
  80.9 3.3 %fusion = f32[256]{0:T(256)S(1)} fusion(bf16[256,8192]{1,0:T(8,128)(2,1)} %all-gather.2.cloned.1.call-done), kind=kLoop, calls=%fused_computation.2 | loop fusion | flops 6291200 | bytes 4195328 | tf_op jit(solution)/shard_map/reduce_sum | solution.py:267
  84.2 0.2 copy-done.3
  84.4 0.0 copy-start.8
  84.4 0.0 copy-start.9
  84.4 1.1 fusion.1.normed_ref
  85.5 0.5 copy-done.8
  85.9 0.6 copy-done.9
  86.6 0.0 copy-start
  86.6 2.0 %fusion.33.k_ref.v_ref = bf16[256,256]{1,0:T(8,128)(2,1)} fusion(bf16[256,8192]{1,0:T(8,128)(2,1)S(1)} %fusion.1.normed_ref, bf16[8192,128]{1,0:T(8,128)(2,1)S(1)} %copy-done.8, bf16[8192,128]{1,0:T(8,128)(2,1)S(1)} %copy-done.9), kind=kOutput, calls=%fused_computation.29 | convolution fusion | flops 1082195968 | bytes 8519680 | tf_op jit(solution)/shard_map/dot_general | solution.py:269
  88.6 0.0 copy-done
  88.6 9.5 %shard_map.103 = (bf16[256,1024]{1,0:T(8,128)(2,1)}, bf16[256,256]{1,0:T(8,128)(2,1)}) custom-call(bf16[256,1024]{1,0:T(8,128)(2,1)} %fusion.30.q_ref, bf16[256,256]{1,0:T(8,128)(2,1)} %fusion.33.k_ref.v_ref, bf16[256,256]{1,0:T(8,128)(2,1)} %fusion.33.k_ref.v_ref, bf16[256,1024]{1,0:T(8,128)(2,1)} %fusion.27.u_ref, f32[256,1]{1,0:T(8,128)} %copy.13.scale_ref, ...), custom_call_target="tpu_custom_call" | custom-call | tf_op jit(solution)/shard_map/pallas_call | solution.py:123
  98.0 0.0 copy-start.1
  98.0 2.2 %copy-done.1 = bf16[256,8192]{1,0:T(8,128)(2,1)S(1)} copy-done((bf16[256,8192]{1,0:T(8,128)(2,1)S(1)}, bf16[256,8192]{1,0:T(8,128)(2,1)}, u32[]{:S(2)}) %copy-start.1) | copy-done | bytes 4194328
  100.2 0.0 copy-start.2
  100.2 0.9 copy-done.2
  101.1 63.7 %shard_map.104 = (f32[1024,128]{1,0:T(8,128)S(1)}, f32[1024,128]{1,0:T(8,128)S(1)}) custom-call(bf16[256,8192]{1,0:T(8,128)(2,1)S(1)} %copy-done.1, bf16[256,256]{1,0:T(8,128)(2,1)S(1)} %copy-done.2), custom_call_target="tpu_custom_call" | custom-call | tf_op jit(solution)/shard_map/pallas_call | solution.py:222
  164.9 0.8 copy.17
  165.7 0.8 copy.18
  (10 shorter events, 0.1 us)
Async XLA Ops:
  7.2 73.7 %all-gather.2.cloned.1.call-start = ((), (), s32[]{:S(2)}) async-start(), calls=%async_computation | async-start | bytes 5242880 | tf_op jit(solution)/shard_map/all_gather | solution.py:261
  12.9 27.3 %collective-permute-start.2 = (bf16[128,2048]{1,0:T(8,128)(2,1)S(1)}, bf16[128,2048]{1,0:T(8,128)(2,1)}, u32[]{:S(2)}, u32[]{:S(2)}) collective-permute-start(bf16[128,2048]{1,0:T(8,128)(2,1)S(1)} %get-tuple-element.15), channel_id=1, source_target_pairs={{0,4},{4,8},{8,12},{12,16},{16,20},{20,24},{24,28},{1,5},{5,9},{9,... | collective-permute-start | bytes 1572872 | tf_op jit(solution)/shard_map/ppermute | solution.py:23
  18.6 21.6 %collective-permute-start.3 = (bf16[128,2048]{1,0:T(8,128)(2,1)S(1)}, bf16[128,2048]{1,0:T(8,128)(2,1)}, u32[]{:S(2)}, u32[]{:S(2)}) collective-permute-start(bf16[128,2048]{1,0:T(8,128)(2,1)S(1)} %get-tuple-element.16), channel_id=1, source_target_pairs={{4,0},{8,4},{12,8},{16,12},{20,16},{24,20},{28,24},{5,1},{9,5},{13... | collective-permute-start | bytes 1572872 | tf_op jit(solution)/shard_map/ppermute | solution.py:23
  21.9 36.1 %copy-start.6 = (s32[256]{0:T(256)}, s32[256]{0:T(256)S(1)}, u32[]{:S(2)}) copy-start(s32[256]{0:T(256)S(1)} %get-tuple-element.11) | copy-start | bytes 3076
  21.9 22.1 %copy-start.4 = (bf16[512,1024]{1,0:T(8,128)(2,1)S(1)}, bf16[512,1024]{1,0:T(8,128)(2,1)}, u32[]{:S(2)}) copy-start(bf16[512,1024]{1,0:T(8,128)(2,1)} %param.10) | copy-start | bytes 3145732
  21.9 28.0 %copy-start.5 = (bf16[512,1024]{1,0:T(8,128)(2,1)S(1)}, bf16[512,1024]{1,0:T(8,128)(2,1)}, u32[]{:S(2)}) copy-start(bf16[512,1024]{1,0:T(8,128)(2,1)} %param.9) | copy-start | bytes 3145732
  44.0 13.0 %copy-start.7 = (f32[8,8]{1,0:T(8,128)S(1)}, f32[8,8]{1,0:T(8,128)}, u32[]{:S(2)}) copy-start(f32[8,8]{1,0:T(8,128)} %param.14) | copy-start | bytes 772
  44.1 14.7 %collective-permute-start.4 = (bf16[128,1024]{1,0:T(8,128)(2,1)S(1)}, bf16[128,1024]{1,0:T(8,128)(2,1)S(1)}, u32[]{:S(2)}, u32[]{:S(2)}) collective-permute-start(bf16[128,1024]{1,0:T(8,128)(2,1)S(1)} %get-tuple-element.17), channel_id=1, source_target_pairs={{0,4},{4,8},{8,12},{12,16},{16,20},{20,24},{24,28},{1,5},{5,9},{9,... | collective-permute-start | bytes 786440 | tf_op jit(solution)/shard_map/ppermute | solution.py:23
  48.6 10.6 %collective-permute-start.5 = (bf16[128,1024]{1,0:T(8,128)(2,1)S(1)}, bf16[128,1024]{1,0:T(8,128)(2,1)}, u32[]{:S(2)}, u32[]{:S(2)}) collective-permute-start(bf16[128,1024]{1,0:T(8,128)(2,1)S(1)} %get-tuple-element.18), channel_id=1, source_target_pairs={{4,0},{8,4},{12,8},{16,12},{20,16},{24,20},{28,24},{5,1},{9,5},{13... | collective-permute-start | bytes 786440 | tf_op jit(solution)/shard_map/ppermute | solution.py:23
  50.0 20.5 %collective-permute-start = (bf16[128,1024]{1,0:T(8,128)(2,1)S(1)}, bf16[128,1024]{1,0:T(8,128)(2,1)}, u32[]{:S(2)}, u32[]{:S(2)}) collective-permute-start(bf16[128,1024]{1,0:T(8,128)(2,1)S(1)} %get-tuple-element.19), channel_id=1, source_target_pairs={{0,4},{4,8},{8,12},{12,16},{16,20},{20,24},{24,28},{1,5},{5,9},{9,... | collective-permute-start | bytes 786440 | tf_op jit(solution)/shard_map/ppermute | solution.py:23
  55.7 14.9 %collective-permute-start.1 = (bf16[128,1024]{1,0:T(8,128)(2,1)S(1)}, bf16[128,1024]{1,0:T(8,128)(2,1)}, u32[]{:S(2)}, u32[]{:S(2)}) collective-permute-start(bf16[128,1024]{1,0:T(8,128)(2,1)S(1)} %get-tuple-element.20), channel_id=1, source_target_pairs={{4,0},{8,4},{12,8},{16,12},{20,16},{24,20},{28,24},{5,1},{9,5},{13... | collective-permute-start | bytes 786440 | tf_op jit(solution)/shard_map/ppermute | solution.py:23
  80.9 3.4 %copy-start.3 = (bf16[256,8192]{1,0:T(8,128)(2,1)S(1)}, bf16[256,8192]{1,0:T(8,128)(2,1)}, u32[]{:S(2)}) copy-start(bf16[256,8192]{1,0:T(8,128)(2,1)} %all-gather.2.cloned.1.call-done) | copy-start | bytes 12582916
  84.4 1.6 copy-start.8
  84.4 2.2 %copy-start.9 = (bf16[8192,128]{1,0:T(8,128)(2,1)S(1)}, bf16[8192,128]{1,0:T(8,128)(2,1)}, u32[]{:S(2)}) copy-start(bf16[8192,128]{1,0:T(8,128)(2,1)} %param.11) | copy-start | bytes 6291460
  86.6 2.0 %copy-start = (bf16[256,8192]{1,0:T(8,128)(2,1)}, bf16[256,8192]{1,0:T(8,128)(2,1)S(1)}, u32[]{:S(2)}) copy-start(bf16[256,8192]{1,0:T(8,128)(2,1)S(1)} %fusion.1.normed_ref) | copy-start | bytes 12582916
  98.0 2.2 %copy-start.1 = (bf16[256,8192]{1,0:T(8,128)(2,1)S(1)}, bf16[256,8192]{1,0:T(8,128)(2,1)}, u32[]{:S(2)}) copy-start(bf16[256,8192]{1,0:T(8,128)(2,1)} %copy-done) | copy-start | bytes 12582916
  100.2 0.9 copy-start.2
Sparse Core Ops, SparseCore 0:
  44.1 36.7 all-gather.1

commit v3 on v2

--- a/solution.py
+++ b/solution.py
@@ -12,15 +12,10 @@
 CAP_L = 256
 PIECE = 128
 LAST_START = CAP_R - PIECE
+CHUNKS = 4
 
 epsilon = 1e-06
 masked_score = -1e30
-
-
-def passed_along(value, axis, steps):
-    count = lax.axis_size(axis)
-    first, last = (max(0, -steps), min(count, count - steps))
-    return lax.ppermute(value, axis, [(source, source + steps) for source in range(first, last)])
 
 
 def derive_moves(lengths):
@@ -142,6 +137,186 @@
     )(queries, keys_values, keys_values, upstream, scales[:, None], segments[:, None], segments[None, :])
 
 
+def front_kernel(dp_count, hidden_ref, query_ref, upstream_ref, hidden_later, query_later, upstream_later,
+                 pick_ref, normed_ref, query_out, upstream_out, full, left_h, right_h, left_q, right_q,
+                 left_u, right_u, right_sent, left_got, left_sent, right_got, mp_sent, mp_got):
+    device, me = lax.axis_index("dp"), lax.axis_index("mp")
+    half, core = me // 2, me % 2
+    near, far, corner = half * 2 + 1 - core, (1 - half) * 2 + core, (1 - half) * 2 + 1 - core
+    has_left, has_right = device > 0, device < dp_count - 1
+    mesh_id = pl.DeviceIdType.MESH
+    width = hidden_ref.shape[1]
+    chunk = width // CHUNKS
+    parts = []
+    for array, later, from_left, from_right in (
+        (hidden_ref, hidden_later, left_h, right_h),
+        (query_ref, query_later, left_q, right_q),
+        (upstream_ref, upstream_later, left_u, right_u),
+    ):
+        for at in range(0, array.shape[1], chunk):
+            parts.append((array, later, from_left, from_right, slice(at, at + chunk)))
+
+    def to_right(p):
+        _, later, from_left, _, columns = parts[p]
+        return pltpu.make_async_remote_copy(
+            src_ref=later.at[:, columns], dst_ref=from_left.at[:, columns],
+            send_sem=right_sent.at[p], recv_sem=left_got.at[p],
+            device_id={"dp": device + 1}, device_id_type=mesh_id,
+        )
+
+    def to_left(p):
+        array, _, _, from_right, columns = parts[p]
+        return pltpu.make_async_remote_copy(
+            src_ref=array.at[:PIECE, columns], dst_ref=from_right.at[:, columns],
+            send_sem=left_sent.at[p], recv_sem=right_got.at[p],
+            device_id={"dp": device - 1}, device_id_type=mesh_id,
+        )
+
+    def over_mp(kind, c):
+        owner, target = ((me, near), (me, far), (far, near))[kind]
+        columns = slice(c * chunk, (c + 1) * chunk)
+        return pltpu.make_async_remote_copy(
+            src_ref=full.at[owner, :, columns], dst_ref=full.at[owner, :, columns],
+            send_sem=mp_sent.at[kind, c], recv_sem=mp_got.at[kind, c],
+            device_id={"mp": target}, device_id_type=mesh_id,
+        )
+
+    def settled(p):
+        array, _, from_left, from_right, columns = parts[p]
+
+        @pl.when(has_left)
+        def _():
+            to_right(p).wait_recv()
+
+        @pl.when(has_right)
+        def _():
+            to_left(p).wait_recv()
+
+        own = PIECE + CAP_R
+        total = jnp.dot(pick_ref[:, :PIECE], from_left[:, columns], preferred_element_type=jnp.float32)
+        total += jnp.dot(pick_ref[:, PIECE:own], array[:, columns], preferred_element_type=jnp.float32)
+        total += jnp.dot(pick_ref[:, own:], from_right[:, columns], preferred_element_type=jnp.float32)
+        return total.astype(jnp.bfloat16)
+
+    barrier = pltpu.get_barrier_semaphore()
+    for target in (near, far):
+        pl.semaphore_signal(barrier, inc=1, device_id={"mp": target}, device_id_type=mesh_id)
+
+    @pl.when(has_left)
+    def _():
+        pl.semaphore_signal(barrier, inc=1, device_id={"dp": device - 1}, device_id_type=mesh_id)
+
+    @pl.when(has_right)
+    def _():
+        pl.semaphore_signal(barrier, inc=1, device_id={"dp": device + 1}, device_id_type=mesh_id)
+
+    @pl.when(has_left & has_right)
+    def _():
+        pl.semaphore_wait(barrier, 4)
+
+    @pl.when(jnp.logical_not(has_left & has_right))
+    def _():
+        pl.semaphore_wait(barrier, 3)
+
+    @pl.when(has_right)
+    def _():
+        for p in range(len(parts)):
+            to_right(p).start()
+
+    @pl.when(has_left)
+    def _():
+        for p in range(len(parts)):
+            to_left(p).start()
+
+    @pl.when(jnp.logical_not(has_left))
+    def _():
+        for ref in (left_h, left_q, left_u):
+            ref[...] = jnp.zeros_like(ref)
+
+    @pl.when(jnp.logical_not(has_right))
+    def _():
+        for ref in (right_h, right_q, right_u):
+            ref[...] = jnp.zeros_like(ref)
+
+    for c in range(CHUNKS):
+        full[me, :, c * chunk : (c + 1) * chunk] = settled(c)
+        over_mp(1, c).start()
+        over_mp(0, c).start()
+        if c > 0:
+            over_mp(1, c - 1).wait_recv()
+            over_mp(2, c - 1).start()
+    for p in range(CHUNKS, len(parts)):
+        target = query_out if parts[p][0] is query_ref else upstream_out
+        target[:, parts[p][4]] = settled(p)
+        if p == CHUNKS:
+            over_mp(1, CHUNKS - 1).wait_recv()
+            over_mp(2, CHUNKS - 1).start()
+    for c in range(CHUNKS):
+        over_mp(0, c).wait_recv()
+        over_mp(2, c).wait_recv()
+
+    owners, rows, _ = full.shape
+    tile = 256
+    squares = jnp.zeros((rows, HD), jnp.float32)
+    for owner in range(owners):
+        for at in range(0, width, HD):
+            wide = full[owner, :, at : at + HD].astype(jnp.float32)
+            squares += wide * wide
+    scale = lax.rsqrt(jnp.sum(squares, axis=1, keepdims=True) / (owners * width) + epsilon)
+    for owner in range(owners):
+        for at in range(0, width, tile):
+            wide = full[owner, :, at : at + tile].astype(jnp.float32)
+            spot = owner * width + at
+            normed_ref[:, spot : spot + tile] = (wide * scale).astype(jnp.bfloat16)
+
+    @pl.when(has_right)
+    def _():
+        for p in range(len(parts)):
+            to_right(p).wait_send()
+
+    @pl.when(has_left)
+    def _():
+        for p in range(len(parts)):
+            to_left(p).wait_send()
+
+    for kind in range(3):
+        for c in range(CHUNKS):
+            over_mp(kind, c).wait_send()
+
+
+def front(hidden, queries, upstream, own_piece, pick):
+    width, head_width = hidden.shape[1], queries.shape[1]
+    owners = lax.axis_size("mp")
+    laters = [
+        lax.dynamic_slice_in_dim(array, own_piece, PIECE, 0) for array in (hidden, queries, upstream)
+    ]
+    part_count = CHUNKS + 2 * (head_width * CHUNKS // width)
+    vmem = pl.BlockSpec(memory_space=pltpu.VMEM)
+    piece = lambda columns: pltpu.VMEM((PIECE, columns), jnp.bfloat16)
+    part_sems = pltpu.SemaphoreType.DMA((part_count,))
+    mp_sems = pltpu.SemaphoreType.DMA((3, CHUNKS))
+    return pl.pallas_call(
+        functools.partial(front_kernel, lax.axis_size("dp")),
+        in_specs=[vmem] * 7,
+        out_specs=[vmem] * 3,
+        out_shape=[
+            jax.ShapeDtypeStruct((CAP_L, owners * width), jnp.bfloat16),
+            jax.ShapeDtypeStruct((CAP_L, head_width), jnp.bfloat16),
+            jax.ShapeDtypeStruct((CAP_L, head_width), jnp.bfloat16),
+        ],
+        scratch_shapes=[
+            pltpu.VMEM((owners, CAP_L, width), jnp.bfloat16),
+            piece(width), piece(width),
+            piece(head_width), piece(head_width),
+            piece(head_width), piece(head_width),
+            part_sems, part_sems, part_sems, part_sems, mp_sems, mp_sems,
+        ],
+        compiler_params=pltpu.CompilerParams(
+            collective_id=1, has_side_effects=True, vmem_limit_bytes=40 * 1024 * 1024
+        ),
+    )(hidden, queries, upstream, *laters, pick)
+
+
 def gradient_kernel(count, normed_ref, cots_ref, key_ref, value_ref, pair_out, pair_in, line_out,
                     line_in, acc, pair_sent, pair_got, line_sent, line_got):
     me = lax.axis_index("dp")
@@ -247,25 +422,8 @@
     positions = jnp.arange(2 * PIECE + CAP_R, dtype=jnp.int32)
     pick = (source[:, None] == positions[None, :]).astype(jnp.bfloat16)
 
-    def exchanged(array):
-        later = lax.dynamic_slice_in_dim(array, own_piece, PIECE, 0)
-        return passed_along(later, "dp", 1), passed_along(array[:PIECE], "dp", -1)
-
-    def settled(array, pieces):
-        pool = jnp.concatenate([pieces[0], array, pieces[1]], axis=0)
-        return jnp.dot(pick, pool, preferred_element_type=jnp.float32).astype(jnp.bfloat16)
-
-    hidden_pieces = exchanged(hidden)
-    query_pieces = exchanged(queries)
-    upstream_pieces = exchanged(upstream)
-    full = lax.all_gather(settled(hidden, hidden_pieces), "mp", axis=1, tiled=True)
-    query_rows = settled(queries, query_pieces)
-    upstream_rows = settled(upstream, upstream_pieces)
+    normed, query_rows, upstream_rows = front(hidden, queries, upstream, own_piece, pick)
     weight = jnp.concatenate([key_weight, value_weight], axis=1)
-    widened = full.astype(jnp.float32)
-    normed = (
-        widened * lax.rsqrt(jnp.mean(widened * widened, axis=1, keepdims=True) + epsilon)
-    ).astype(jnp.bfloat16)
     keys_values = jnp.dot(normed, weight, preferred_element_type=jnp.float32).astype(jnp.bfloat16)
     attention_out, cots = attend(query_rows, keys_values, upstream_rows, scales, segments)
     key_grad, value_grad = gradient_sum(normed, cots)

time: 174 us -> 154 us (0.89)
  Pallas kernels: 73.2 us -> 131 us
  waiting for transfers between devices: 35.6 us -> 0 us
  starting transfers between devices: 19.7 us -> 0 us
  between operations: 16.2 us -> 2.74 us
  matrix products: 10.6 us -> 2.27 us
  other arithmetic: 8.08 us -> 3.98 us
  local copies, waits for them, and re-layouts: 9.95 us -> 13.6 us
    pallas_call x0 -> x1, Pallas kernels: none -> 48.4 us  [front(): pl.pallas_call(functools.partial(front_kernel, lax.axis_size('dp')), in_s...]
    ppermute x6 -> x0, waiting for transfers between devices: 27.6 us -> none  [passed_along(): lax.ppermute(value, axis, [(source, source + steps) for source in range(f...]
    ppermute x6 -> x0, starting transfers between devices: 19.7 us -> none  [passed_along(): lax.ppermute(value, axis, [(source, source + steps) for source in range(f...]
    pallas_call x1, Pallas kernels: 63.7 us -> 72.7 us  [gradient_sum(): pl.pallas_call(functools.partial(gradient_kernel, count), in_specs=[vmem,...]
    dot_general x3 -> x0, matrix products: 8.64 us -> none  [settled(): jnp.dot(pick, pool, preferred_element_type=jnp.float32).astype(jnp.bfloat16)]
    all_gather x1 -> x0, waiting for transfers between devices: 7.92 us -> none  [body(): lax.all_gather(settled(hidden, hidden_pieces), 'mp', axis=1, tiled=True)]
    reduce_sum x1 -> x0, other arithmetic: 3.25 us -> none  [body(): jnp.mean(widened * widened, axis=1, keepdims=True) + epsilon]
    unnamed x22 -> x26, local copies, waits for them, and re-layouts: 5.98 us -> 8.75 us
  transfers between devices with their start and end apart: 7 -> 0, of which waited for: 4 -> 0; matrix products, arithmetic and copies ran while one was open for 5% -> 0% of each run, Pallas kernels for 0% -> 0%
where the time goes in v3:
time: 154 us; the launch traced here: 153 us
  Pallas kernels  131 us (85%)
  local copies, waits for them, and re-layouts  13.6 us (9%)
  other arithmetic  3.98 us (3%)
  between operations  2.74 us (2%)
  matrix products  2.27 us (1%)
    pallas_call x1, Pallas kernels, gradient_sum(): pl.pallas_call(functools.partial(gradient_kernel, count), in_specs=[vmem,...  72.7 us
    pallas_call x1, Pallas kernels, front(): pl.pallas_call(functools.partial(front_kernel, lax.axis_size('dp')), in_s...  48.4 us
    pallas_call x1, Pallas kernels, attend(): pl.pallas_call(attention_kernel, grid=(width // HD,), in_specs=[head_bloc...  9.47 us
    unnamed x26, local copies, waits for them, and re-layouts  8.75 us

profile of v3, /device:TPU:0, one launch (start us, length us, event | category | flops | bytes accessed | tf_op | source)
XLA Modules:
  0.0 153.2 jit_solution(14020855360477841183)
XLA Ops:
  0.6 0.0 copy-start.10
  0.6 1.0 convert_reduce_fusion.1
  1.6 0.1 select_add_fusion
  1.7 0.9 select_select_fusion
  2.6 0.8 multiply_reduce_fusion
  3.3 0.1 bitcast_subtract_fusion
  3.5 0.8 fusion.11
  4.2 0.1 broadcast_in_dim.86
  4.3 0.1 select_reduce_fusion.2
  4.4 0.1 reshape.157
  4.5 0.1 convert_reduce_fusion
  4.6 0.0 copy-start.8
  4.6 0.1 fusion.7.pick_ref
  4.7 0.6 dynamic_slice.25
  7.3 1.2 constant_dynamic-slice_fusion
  8.5 1.2 constant_dynamic-slice_fusion.2.hidden_later
  9.7 0.0 copy-start.2
  9.7 1.6 %copy-done.2 = bf16[512,2048]{1,0:T(8,128)(2,1)S(1)} copy-done((bf16[512,2048]{1,0:T(8,128)(2,1)S(1)}, bf16[512,2048]{1,0:T(8,128)(2,1)}, u32[]{:S(2)}) %copy-start.2) | copy-done | bytes 2097176
  11.3 0.0 copy-start.3
  11.3 1.2 copy-done.3
  12.5 0.0 copy-start.4
  12.5 1.2 copy-done.4
  13.7 0.0 copy-start.11
  13.7 48.4 %shard_map.103 = (bf16[256,8192]{1,0:T(8,128)(2,1)S(1)}, bf16[256,1024]{1,0:T(8,128)(2,1)S(1)}, bf16[256,1024]{1,0:T(8,128)(2,1)S(1)}) custom-call(bf16[512,2048]{1,0:T(8,128)(2,1)S(1)} %copy-done.2, bf16[512,1024]{1,0:T(8,128)(2,1)S(1)} %copy-done.3, bf16[512,1024]{1,0:T(8,128)(2,1)S(1)} %copy-done.4, ...), custom_call_target="tpu_custom_call" | custom-call | tf_op jit(solution)/shard_map/pallas_call | solution.py:298
  62.1 0.0 copy-start
  62.1 0.0 copy-start.5
  62.1 0.0 copy-start.6
  62.1 0.0 copy-done.10
  62.1 0.0 copy-done.11
  62.2 0.0 copy-start.9
  62.2 2.3 %fusion.4.k_ref.v_ref = bf16[256,256]{1,0:T(8,128)(2,1)} fusion(bf16[256,8192]{1,0:T(8,128)(2,1)S(1)} %get-tuple-element.11.normed_ref, bf16[8192,128]{1,0:T(8,128)(2,1)S(1)} %copy-done.10, bf16[8192,128]{1,0:T(8,128)(2,1)S(1)} %copy-done.11), kind=kOutput, calls=%fused_computation.4 | convolution fusion | flops 1082195968 | bytes 8519680 | tf_op jit(solution)/shard_map/dot_general | solution.py:427
  64.4 0.0 copy-done
  64.4 0.0 copy-done.5
  64.4 0.0 copy-done.6
  64.4 0.0 copy-done.9
  64.5 0.1 reshape.158
  64.6 0.1 select_reduce_fusion
  64.7 0.8 copy.13.scale_ref
  65.5 0.0 copy-done.8
  65.5 0.8 copy.14.seg_col_ref
  66.3 9.5 %shard_map.104 = (bf16[256,1024]{1,0:T(8,128)(2,1)}, bf16[256,256]{1,0:T(8,128)(2,1)}) custom-call(bf16[256,1024]{1,0:T(8,128)(2,1)} %copy-done.5, bf16[256,256]{1,0:T(8,128)(2,1)} %fusion.4.k_ref.v_ref, bf16[256,256]{1,0:T(8,128)(2,1)} %fusion.4.k_ref.v_ref, bf16[256,1024]{1,0:T(8,128)(2,1)} %copy-done.6, f32[256,1]{1,0:T(8,128)} %copy.13.scale_ref, ...), custom_call_target="tpu_custom_call" | custom-call | tf_op jit(solution)/shard_map/pallas_call | solution.py:118
  75.8 0.0 copy-start.1
  75.8 2.2 %copy-done.1 = bf16[256,8192]{1,0:T(8,128)(2,1)S(1)} copy-done((bf16[256,8192]{1,0:T(8,128)(2,1)S(1)}, bf16[256,8192]{1,0:T(8,128)(2,1)}, u32[]{:S(2)}) %copy-start.1) | copy-done | bytes 4194328
  77.9 0.0 copy-start.7
  78.0 0.9 copy-done.7
  78.9 72.7 %shard_map.105 = (f32[1024,128]{1,0:T(8,128)S(1)}, f32[1024,128]{1,0:T(8,128)S(1)}) custom-call(bf16[256,8192]{1,0:T(8,128)(2,1)S(1)} %copy-done.1, bf16[256,256]{1,0:T(8,128)(2,1)S(1)} %copy-done.7), custom_call_target="tpu_custom_call" | custom-call | tf_op jit(solution)/shard_map/pallas_call | solution.py:397
  151.6 0.8 copy.17
  152.4 0.8 copy.18
  (9 shorter events, 0.1 us)
Async XLA Ops:
  0.6 61.5 %copy-start.10 = (bf16[8192,128]{1,0:T(8,128)(2,1)S(1)}, bf16[8192,128]{1,0:T(8,128)(2,1)}, u32[]{:S(2)}) copy-start(bf16[8192,128]{1,0:T(8,128)(2,1)} %param.12) | copy-start | bytes 6291460
  4.6 60.9 %copy-start.8 = (s32[256]{0:T(256)}, s32[256]{0:T(256)S(1)}, u32[]{:S(2)}) copy-start(s32[256]{0:T(256)S(1)} %get-tuple-element.17) | copy-start | bytes 3076
  9.7 1.6 %copy-start.2 = (bf16[512,2048]{1,0:T(8,128)(2,1)S(1)}, bf16[512,2048]{1,0:T(8,128)(2,1)}, u32[]{:S(2)}) copy-start(bf16[512,2048]{1,0:T(8,128)(2,1)} %hidden_ref.1) | copy-start | bytes 6291460
  11.3 1.2 copy-start.3
  12.5 1.2 copy-start.4
  13.7 48.4 %copy-start.11 = (bf16[8192,128]{1,0:T(8,128)(2,1)S(1)}, bf16[8192,128]{1,0:T(8,128)(2,1)}, u32[]{:S(2)}) copy-start(bf16[8192,128]{1,0:T(8,128)(2,1)} %param.11) | copy-start | bytes 6291460
  62.1 2.3 %copy-start = (bf16[256,8192]{1,0:T(8,128)(2,1)}, bf16[256,8192]{1,0:T(8,128)(2,1)S(1)}, u32[]{:S(2)}) copy-start(bf16[256,8192]{1,0:T(8,128)(2,1)S(1)} %get-tuple-element.11.normed_ref) | copy-start | bytes 12582916
  62.1 2.3 %copy-start.5 = (bf16[256,1024]{1,0:T(8,128)(2,1)}, bf16[256,1024]{1,0:T(8,128)(2,1)S(1)}, u32[]{:S(2)}) copy-start(bf16[256,1024]{1,0:T(8,128)(2,1)S(1)} %get-tuple-element.10.q_ref) | copy-start | bytes 1572868
  62.1 2.3 %copy-start.6 = (bf16[256,1024]{1,0:T(8,128)(2,1)}, bf16[256,1024]{1,0:T(8,128)(2,1)S(1)}, u32[]{:S(2)}) copy-start(bf16[256,1024]{1,0:T(8,128)(2,1)S(1)} %get-tuple-element.12.u_ref) | copy-start | bytes 1572868
  62.2 2.3 %copy-start.9 = (f32[8,8]{1,0:T(8,128)S(1)}, f32[8,8]{1,0:T(8,128)}, u32[]{:S(2)}) copy-start(f32[8,8]{1,0:T(8,128)} %param.14) | copy-start | bytes 772
  75.8 2.2 %copy-start.1 = (bf16[256,8192]{1,0:T(8,128)(2,1)S(1)}, bf16[256,8192]{1,0:T(8,128)(2,1)}, u32[]{:S(2)}) copy-start(bf16[256,8192]{1,0:T(8,128)(2,1)} %copy-done) | copy-start | bytes 12582916
  77.9 0.9 copy-start.7

commit v4 on v3

--- a/solution.py
+++ b/solution.py
@@ -13,6 +13,7 @@
 PIECE = 128
 LAST_START = CAP_R - PIECE
 CHUNKS = 4
+AHEAD = 3
 
 epsilon = 1e-06
 masked_score = -1e30
@@ -137,8 +138,9 @@
     )(queries, keys_values, keys_values, upstream, scales[:, None], segments[:, None], segments[None, :])
 
 
-def front_kernel(dp_count, hidden_ref, query_ref, upstream_ref, hidden_later, query_later, upstream_later,
-                 pick_ref, normed_ref, query_out, upstream_out, full, left_h, right_h, left_q, right_q,
+def front_kernel(dp_count, hidden_hbm, query_hbm, upstream_hbm, key_hbm, value_hbm, hidden_later, query_later,
+                 upstream_later, pick_ref, normed_ref, kv_ref, query_out, upstream_out, hidden_ref, query_ref,
+                 upstream_ref, weight_ref, local_done, full, left_h, right_h, left_q, right_q,
                  left_u, right_u, right_sent, left_got, left_sent, right_got, mp_sent, mp_got):
     device, me = lax.axis_index("dp"), lax.axis_index("mp")
     half, core = me // 2, me % 2
@@ -148,16 +150,26 @@
     width = hidden_ref.shape[1]
     chunk = width // CHUNKS
     parts = []
-    for array, later, from_left, from_right in (
-        (hidden_ref, hidden_later, left_h, right_h),
-        (query_ref, query_later, left_q, right_q),
-        (upstream_ref, upstream_later, left_u, right_u),
+    for array, source, later, from_left, from_right in (
+        (hidden_ref, hidden_hbm, hidden_later, left_h, right_h),
+        (query_ref, query_hbm, query_later, left_q, right_q),
+        (upstream_ref, upstream_hbm, upstream_later, left_u, right_u),
     ):
         for at in range(0, array.shape[1], chunk):
-            parts.append((array, later, from_left, from_right, slice(at, at + chunk)))
+            parts.append((array, later, from_left, from_right, slice(at, at + chunk), source))
+    fetches = [
+        pltpu.make_async_copy(source, target, local_done.at[n])
+        for n, (source, target) in enumerate((
+            (hidden_hbm, hidden_ref),
+            (query_hbm, query_ref),
+            (upstream_hbm, upstream_ref),
+            (key_hbm, weight_ref.at[:, :HD]),
+            (value_hbm, weight_ref.at[:, HD:]),
+        ))
+    ]
 
     def to_right(p):
-        _, later, from_left, _, columns = parts[p]
+        _, later, from_left, _, columns, _ = parts[p]
         return pltpu.make_async_remote_copy(
             src_ref=later.at[:, columns], dst_ref=from_left.at[:, columns],
             send_sem=right_sent.at[p], recv_sem=left_got.at[p],
@@ -165,9 +177,9 @@
         )
 
     def to_left(p):
-        array, _, _, from_right, columns = parts[p]
+        _, _, _, from_right, columns, source = parts[p]
         return pltpu.make_async_remote_copy(
-            src_ref=array.at[:PIECE, columns], dst_ref=from_right.at[:, columns],
+            src_ref=source.at[:PIECE, columns], dst_ref=from_right.at[:, columns],
             send_sem=left_sent.at[p], recv_sem=right_got.at[p],
             device_id={"dp": device - 1}, device_id_type=mesh_id,
         )
@@ -182,7 +194,7 @@
         )
 
     def settled(p):
-        array, _, from_left, from_right, columns = parts[p]
+        array, _, from_left, from_right, columns, _ = parts[p]
 
         @pl.when(has_left)
         def _():
@@ -198,6 +210,8 @@
         total += jnp.dot(pick_ref[:, own:], from_right[:, columns], preferred_element_type=jnp.float32)
         return total.astype(jnp.bfloat16)
 
+    for fetch in fetches:
+        fetch.start()
     barrier = pltpu.get_barrier_semaphore()
     for target in (near, far):
         pl.semaphore_signal(barrier, inc=1, device_id={"mp": target}, device_id_type=mesh_id)
@@ -238,6 +252,7 @@
         for ref in (right_h, right_q, right_u):
             ref[...] = jnp.zeros_like(ref)
 
+    fetches[0].wait()
     for c in range(CHUNKS):
         full[me, :, c * chunk : (c + 1) * chunk] = settled(c)
         over_mp(1, c).start()
@@ -245,12 +260,8 @@
         if c > 0:
             over_mp(1, c - 1).wait_recv()
             over_mp(2, c - 1).start()
-    for p in range(CHUNKS, len(parts)):
-        target = query_out if parts[p][0] is query_ref else upstream_out
-        target[:, parts[p][4]] = settled(p)
-        if p == CHUNKS:
-            over_mp(1, CHUNKS - 1).wait_recv()
-            over_mp(2, CHUNKS - 1).start()
+    over_mp(1, CHUNKS - 1).wait_recv()
+    over_mp(2, CHUNKS - 1).start()
     for c in range(CHUNKS):
         over_mp(0, c).wait_recv()
         over_mp(2, c).wait_recv()
@@ -268,6 +279,16 @@
             wide = full[owner, :, at : at + tile].astype(jnp.float32)
             spot = owner * width + at
             normed_ref[:, spot : spot + tile] = (wide * scale).astype(jnp.bfloat16)
+    fetches[3].wait()
+    fetches[4].wait()
+    kv_ref[...] = jnp.dot(
+        normed_ref[...], weight_ref[...], preferred_element_type=jnp.float32
+    ).astype(jnp.bfloat16)
+    fetches[1].wait()
+    fetches[2].wait()
+    for p in range(CHUNKS, len(parts)):
+        target = query_out if parts[p][0] is query_ref else upstream_out
+        target[:, parts[p][4]] = settled(p)
 
     @pl.when(has_right)
     def _():
@@ -284,7 +305,7 @@
             over_mp(kind, c).wait_send()
 
 
-def front(hidden, queries, upstream, own_piece, pick):
+def front(hidden, queries, upstream, key_weight, value_weight, own_piece, pick):
     width, head_width = hidden.shape[1], queries.shape[1]
     owners = lax.axis_size("mp")
     laters = [
@@ -297,14 +318,20 @@
     mp_sems = pltpu.SemaphoreType.DMA((3, CHUNKS))
     return pl.pallas_call(
         functools.partial(front_kernel, lax.axis_size("dp")),
-        in_specs=[vmem] * 7,
-        out_specs=[vmem] * 3,
+        in_specs=[pl.BlockSpec(memory_space=pl.ANY)] * 5 + [vmem] * 4,
+        out_specs=[vmem] * 4,
         out_shape=[
             jax.ShapeDtypeStruct((CAP_L, owners * width), jnp.bfloat16),
+            jax.ShapeDtypeStruct((CAP_L, 2 * HD), jnp.bfloat16),
             jax.ShapeDtypeStruct((CAP_L, head_width), jnp.bfloat16),
             jax.ShapeDtypeStruct((CAP_L, head_width), jnp.bfloat16),
         ],
         scratch_shapes=[
+            pltpu.VMEM(hidden.shape, jnp.bfloat16),
+            pltpu.VMEM(queries.shape, jnp.bfloat16),
+            pltpu.VMEM(upstream.shape, jnp.bfloat16),
+            pltpu.VMEM((owners * width, 2 * HD), jnp.bfloat16),
+            pltpu.SemaphoreType.DMA((5,)),
             pltpu.VMEM((owners, CAP_L, width), jnp.bfloat16),
             piece(width), piece(width),
             piece(head_width), piece(head_width),
@@ -312,9 +339,9 @@
             part_sems, part_sems, part_sems, part_sems, mp_sems, mp_sems,
         ],
         compiler_params=pltpu.CompilerParams(
-            collective_id=1, has_side_effects=True, vmem_limit_bytes=40 * 1024 * 1024
+            collective_id=1, has_side_effects=True, vmem_limit_bytes=48 * 1024 * 1024
         ),
-    )(hidden, queries, upstream, *laters, pick)
+    )(hidden, queries, upstream, key_weight, value_weight, *laters, pick)
 
 
 def gradient_kernel(count, normed_ref, cots_ref, key_ref, value_ref, pair_out, pair_in, line_out,
@@ -322,15 +349,17 @@
     me = lax.axis_index("dp")
     lines = count // 2
     line, side = me // 2, me % 2
-    width = acc.shape[1]
+    width = acc.shape[2]
     mesh_id = pl.DeviceIdType.MESH
 
     def place(k):
         return (line + 1 + k) % lines
 
-    def share(owner):
+    def share(p, of_side):
+        owner = place(p // 2) * 2 + of_side
         columns = pl.ds(pl.multiple_of(owner * width, width), width)
-        return jnp.dot(cots_ref[...], normed_ref[:, columns], preferred_element_type=jnp.float32)
+        rows = pl.ds(pl.multiple_of(p % 2 * HD, HD), HD)
+        return jnp.dot(cots_ref[rows], normed_ref[:, columns], preferred_element_type=jnp.float32)
 
     def pair_copy(k):
         return pltpu.make_async_remote_copy(
@@ -343,7 +372,7 @@
         return pltpu.make_async_remote_copy(
             src_ref=line_out.at[k], dst_ref=line_in.at[k],
             send_sem=line_sent.at[k], recv_sem=line_got.at[k],
-            device_id={"dp": place(k) * 2 + side}, device_id_type=mesh_id,
+            device_id={"dp": place(k // 2) * 2 + side}, device_id_type=mesh_id,
         )
 
     barrier = pltpu.get_barrier_semaphore()
@@ -354,38 +383,51 @@
         pl.semaphore_signal(barrier, inc=1, device_id={"dp": place(k) * 2 + side}, device_id_type=mesh_id)
 
     pl.semaphore_wait(barrier, lines)
-
-    @pl.loop(0, lines)
-    def _(k):
-        pair_out[k] = share(place(k) * 2 + 1 - side).astype(jnp.bfloat16)
-        pair_copy(k).start()
+    total = 2 * lines
+
+    for p in range(AHEAD):
+        pair_out[p] = share(p, 1 - side).astype(jnp.bfloat16)
+        pair_copy(p).start()
+
+    @pl.loop(0, total - 2)
+    def _(p):
+        own = share(p, side)
+
+        @pl.when(p + AHEAD < total)
+        def _():
+            pair_out[p + AHEAD] = share(p + AHEAD, 1 - side).astype(jnp.bfloat16)
+
+        pair_copy(p).wait_recv()
+
+        @pl.when(p + AHEAD < total)
+        def _():
+            pair_copy(p + AHEAD).start()
+
+        line_out[p] = (own + pair_in[p].astype(jnp.float32)).astype(jnp.bfloat16)
+        line_copy(p).start()
+
+    for h in range(2):
+        acc[h] = share(total - 2 + h, side)
+    for h in range(2):
+        pair_copy(total - 2 + h).wait_recv()
+        acc[h] += pair_in[total - 2 + h].astype(jnp.float32)
 
     @pl.loop(0, lines - 1)
     def _(k):
-        own = share(place(k) * 2 + side)
-        pair_copy(k).wait_recv()
-        line_out[k] = (own + pair_in[k].astype(jnp.float32)).astype(jnp.bfloat16)
-        line_copy(k).start()
-
-    acc[...] = share(me)
-    pair_copy(lines - 1).wait_recv()
-    acc[...] += pair_in[lines - 1].astype(jnp.float32)
-
-    @pl.loop(0, lines - 1)
-    def _(k):
-        line_copy(k).wait_recv()
-        acc[...] += line_in[k].astype(jnp.float32)
-
-    key_ref[...] = acc[:HD].T
-    value_ref[...] = acc[HD:].T
-
-    @pl.loop(0, lines)
-    def _(k):
-        pair_copy(k).wait_send()
-
-    @pl.loop(0, lines - 1)
-    def _(k):
-        line_copy(k).wait_send()
+        for h in range(2):
+            line_copy(2 * k + h).wait_recv()
+            acc[h] += line_in[2 * k + h].astype(jnp.float32)
+
+    key_ref[...] = acc[0].T
+    value_ref[...] = acc[1].T
+
+    @pl.loop(0, total)
+    def _(p):
+        pair_copy(p).wait_send()
+
+    @pl.loop(0, total - 2)
+    def _(p):
+        line_copy(p).wait_send()
 
 
 def gradient_sum(normed, cots):
@@ -393,7 +435,7 @@
     lines = count // 2
     width = normed.shape[1] // count
     vmem = pl.BlockSpec(memory_space=pltpu.VMEM)
-    shares = lambda n: pltpu.VMEM((n, 2 * HD, width), jnp.bfloat16)
+    shares = lambda n: pltpu.VMEM((2 * n, HD, width), jnp.bfloat16)
     return pl.pallas_call(
         functools.partial(gradient_kernel, count),
         in_specs=[vmem, vmem],
@@ -404,11 +446,11 @@
             shares(lines),
             shares(lines - 1),
             shares(lines - 1),
-            pltpu.VMEM((2 * HD, width), jnp.float32),
-            pltpu.SemaphoreType.DMA((lines,)),
-            pltpu.SemaphoreType.DMA((lines,)),
-            pltpu.SemaphoreType.DMA((lines - 1,)),
-            pltpu.SemaphoreType.DMA((lines - 1,)),
+            pltpu.VMEM((2, HD, width), jnp.float32),
+            pltpu.SemaphoreType.DMA((2 * lines,)),
+            pltpu.SemaphoreType.DMA((2 * lines,)),
+            pltpu.SemaphoreType.DMA((2 * lines - 2,)),
+            pltpu.SemaphoreType.DMA((2 * lines - 2,)),
         ],
         compiler_params=pltpu.CompilerParams(
             collective_id=0, has_side_effects=True, vmem_limit_bytes=40 * 1024 * 1024
@@ -422,9 +464,9 @@
     positions = jnp.arange(2 * PIECE + CAP_R, dtype=jnp.int32)
     pick = (source[:, None] == positions[None, :]).astype(jnp.bfloat16)
 
-    normed, query_rows, upstream_rows = front(hidden, queries, upstream, own_piece, pick)
-    weight = jnp.concatenate([key_weight, value_weight], axis=1)
-    keys_values = jnp.dot(normed, weight, preferred_element_type=jnp.float32).astype(jnp.bfloat16)
+    normed, keys_values, query_rows, upstream_rows = front(
+        hidden, queries, upstream, key_weight, value_weight, own_piece, pick
+    )
     attention_out, cots = attend(query_rows, keys_values, upstream_rows, scales, segments)
     key_grad, value_grad = gradient_sum(normed, cots)
     return (attention_out, key_grad, value_grad)

time: 154 us -> 152 us (0.987)
  matrix products: 2.27 us -> 0 us
  Pallas kernels: 131 us -> 133 us
  local copies, waits for them, and re-layouts: 13.6 us -> 11.8 us
    dot_general x1 -> x0, matrix products: 2.27 us -> none  [body(): jnp.dot(normed, weight, preferred_element_type=jnp.float32)]
    pallas_call x1, Pallas kernels: 48.4 us -> 50.5 us  [front(): pl.pallas_call(functools.partial(front_kernel, lax.axis_size('dp')), in_s...]
    unnamed x26 -> x20, local copies, waits for them, and re-layouts: 8.75 us -> 6.92 us
where the time goes in v4:
time: 152 us; the launch traced here: 151 us
  Pallas kernels  133 us (88%)
  local copies, waits for them, and re-layouts  11.8 us (8%)
  other arithmetic  3.98 us (3%)
  between operations  2.72 us (2%)
    pallas_call x1, Pallas kernels, gradient_sum(): pl.pallas_call(functools.partial(gradient_kernel, count), in_specs=[vmem,...  72.9 us
    pallas_call x1, Pallas kernels, front(): pl.pallas_call(functools.partial(front_kernel, lax.axis_size('dp')), in_s...  50.5 us
    pallas_call x1, Pallas kernels, attend(): pl.pallas_call(attention_kernel, grid=(width // HD,), in_specs=[head_bloc...  9.47 us
    unnamed x20, local copies, waits for them, and re-layouts  6.92 us

profile of v4, /device:TPU:0, one launch (start us, length us, event | category | flops | bytes accessed | tf_op | source)
XLA Modules:
  0.0 151.3 jit_solution(14628353795223146517)
XLA Ops:
  0.6 0.0 copy-start.2
  0.6 0.0 copy-start.1
  0.7 0.9 convert_reduce_fusion.1
  1.6 0.1 select_add_fusion
  1.7 0.9 select_select_fusion
  2.6 0.8 multiply_reduce_fusion
  3.4 0.1 bitcast_subtract_fusion
  3.5 0.8 fusion.4
  4.2 0.1 broadcast_in_dim.86
  4.3 0.1 select_reduce_fusion.2
  4.4 0.1 reshape.157
  4.5 0.1 convert_reduce_fusion
  4.6 0.0 copy-start.7
  4.6 0.1 fusion.pick_ref
  4.8 0.6 dynamic_slice.25
  7.3 1.2 constant_dynamic-slice_fusion
  8.5 1.2 constant_dynamic-slice_fusion.2.hidden_later
  9.7 0.0 copy-done.2
  9.7 0.0 copy-done.1
  9.7 0.0 copy-start.8
  9.7 50.5 %shard_map.103 = (bf16[256,8192]{1,0:T(8,128)(2,1)}, bf16[256,256]{1,0:T(8,128)(2,1)S(1)}, bf16[256,1024]{1,0:T(8,128)(2,1)S(1)}, bf16[256,1024]{1,0:T(8,128)(2,1)S(1)}) custom-call(bf16[512,2048]{1,0:T(8,128)(2,1)} %hidden_hbm.1, bf16[512,1024]{1,0:T(8,128)(2,1)S(1)} %copy-done.1, bf16[512,1024]{1,0:T(8,128)(2,1)S(1)} %copy-done.2, ...), custom_call_target="tpu_custom_call" | custom-call | tf_op jit(solution)/shard_map/pallas_call | solution.py:319
  60.2 0.0 copy-start.3
  60.3 0.8 copy-done.3
  61.0 0.0 copy-start.4
  61.0 0.8 copy-done.4
  61.8 0.0 copy-start.5
  61.8 0.6 copy-done.5
  62.5 0.0 copy-done.8
  62.5 0.1 reshape.158
  62.6 0.1 select_reduce_fusion
  62.7 0.8 copy.13.scale_ref
  63.5 0.0 copy-done.7
  63.5 0.8 copy.14.seg_col_ref
  64.3 9.5 %shard_map.104 = (bf16[256,1024]{1,0:T(8,128)(2,1)}, bf16[256,256]{1,0:T(8,128)(2,1)}) custom-call(bf16[256,1024]{1,0:T(8,128)(2,1)} %copy-done.3, bf16[256,256]{1,0:T(8,128)(2,1)} %copy-done.5, bf16[256,256]{1,0:T(8,128)(2,1)} %copy-done.5, bf16[256,1024]{1,0:T(8,128)(2,1)} %copy-done.4, f32[256,1]{1,0:T(8,128)} %copy.13.scale_ref, ...), custom_call_target="tpu_custom_call" | custom-call | tf_op jit(solution)/shard_map/pallas_call | solution.py:119
  73.7 0.0 copy-start
  73.8 2.2 %copy-done = bf16[256,8192]{1,0:T(8,128)(2,1)S(1)} copy-done((bf16[256,8192]{1,0:T(8,128)(2,1)S(1)}, bf16[256,8192]{1,0:T(8,128)(2,1)}, u32[]{:S(2)}) %copy-start) | copy-done | bytes 4194328
  75.9 0.0 copy-start.6
  75.9 0.9 copy-done.6
  76.8 72.9 %shard_map.105 = (f32[1024,128]{1,0:T(8,128)S(1)}, f32[1024,128]{1,0:T(8,128)S(1)}) custom-call(bf16[256,8192]{1,0:T(8,128)(2,1)S(1)} %copy-done, bf16[256,256]{1,0:T(8,128)(2,1)S(1)} %copy-done.6), custom_call_target="tpu_custom_call" | custom-call | tf_op jit(solution)/shard_map/pallas_call | solution.py:439
  149.7 0.8 copy.17
  150.5 0.8 copy.18
  (9 shorter events, 0.1 us)
Async XLA Ops:
  0.6 9.1 %copy-start.2 = (bf16[512,1024]{1,0:T(8,128)(2,1)S(1)}, bf16[512,1024]{1,0:T(8,128)(2,1)}, u32[]{:S(2)}) copy-start(bf16[512,1024]{1,0:T(8,128)(2,1)} %upstream_hbm.1) | copy-start | bytes 3145732
  0.6 9.1 %copy-start.1 = (bf16[512,1024]{1,0:T(8,128)(2,1)S(1)}, bf16[512,1024]{1,0:T(8,128)(2,1)}, u32[]{:S(2)}) copy-start(bf16[512,1024]{1,0:T(8,128)(2,1)} %query_hbm.1) | copy-start | bytes 3145732
  4.6 58.9 %copy-start.7 = (s32[256]{0:T(256)}, s32[256]{0:T(256)S(1)}, u32[]{:S(2)}) copy-start(s32[256]{0:T(256)S(1)} %get-tuple-element.19) | copy-start | bytes 3076
  9.7 52.8 %copy-start.8 = (f32[8,8]{1,0:T(8,128)S(1)}, f32[8,8]{1,0:T(8,128)}, u32[]{:S(2)}) copy-start(f32[8,8]{1,0:T(8,128)} %param.14) | copy-start | bytes 772
  60.2 0.8 copy-start.3
  61.0 0.8 copy-start.4
  61.8 0.6 copy-start.5
  73.7 2.2 %copy-start = (bf16[256,8192]{1,0:T(8,128)(2,1)S(1)}, bf16[256,8192]{1,0:T(8,128)(2,1)}, u32[]{:S(2)}) copy-start(bf16[256,8192]{1,0:T(8,128)(2,1)} %get-tuple-element.15.normed_ref) | copy-start | bytes 12582916
  75.9 0.9 copy-start.6

commit v5 on v4

--- a/solution.py
+++ b/solution.py
@@ -232,15 +232,18 @@
     def _():
         pl.semaphore_wait(barrier, 3)
 
-    @pl.when(has_right)
-    def _():
-        for p in range(len(parts)):
-            to_right(p).start()
-
-    @pl.when(has_left)
-    def _():
-        for p in range(len(parts)):
-            to_left(p).start()
+    def send(these):
+        @pl.when(has_right)
+        def _():
+            for p in these:
+                to_right(p).start()
+
+        @pl.when(has_left)
+        def _():
+            for p in these:
+                to_left(p).start()
+
+    send(range(CHUNKS))
 
     @pl.when(jnp.logical_not(has_left))
     def _():
@@ -255,6 +258,7 @@
     fetches[0].wait()
     for c in range(CHUNKS):
         full[me, :, c * chunk : (c + 1) * chunk] = settled(c)
+        send(range(CHUNKS + c, len(parts), CHUNKS))
         over_mp(1, c).start()
         over_mp(0, c).start()
         if c > 0:

time: 152 us -> 144 us (0.947)
  Pallas kernels: 133 us -> 124 us
    pallas_call x1, Pallas kernels: 72.9 us -> 64.3 us  [gradient_sum(): pl.pallas_call(functools.partial(gradient_kernel, count), in_specs=[vmem,...]
where the time goes in v5:
time: 144 us; the launch traced here: 143 us
  Pallas kernels  124 us (86%)
  local copies, waits for them, and re-layouts  11.8 us (8%)
  other arithmetic  3.98 us (3%)
  between operations  2.72 us (2%)
    pallas_call x1, Pallas kernels, gradient_sum(): pl.pallas_call(functools.partial(gradient_kernel, count), in_specs=[vmem,...  64.3 us
    pallas_call x1, Pallas kernels, front(): pl.pallas_call(functools.partial(front_kernel, lax.axis_size('dp')), in_s...  50.5 us
    pallas_call x1, Pallas kernels, attend(): pl.pallas_call(attention_kernel, grid=(width // HD,), in_specs=[head_bloc...  9.47 us
    unnamed x20, local copies, waits for them, and re-layouts  6.92 us

profile of v5, /device:TPU:0, one launch (start us, length us, event | category | flops | bytes accessed | tf_op | source)
XLA Modules:
  0.0 142.7 jit_solution(7730855633342052411)
XLA Ops:
  0.6 0.0 copy-start.2
  0.6 0.0 copy-start.1
  0.7 0.9 convert_reduce_fusion.1
  1.6 0.1 select_add_fusion
  1.7 0.9 select_select_fusion
  2.6 0.8 multiply_reduce_fusion
  3.4 0.1 bitcast_subtract_fusion
  3.5 0.8 fusion.4
  4.2 0.1 broadcast_in_dim.86
  4.3 0.1 select_reduce_fusion.2
  4.4 0.1 reshape.157
  4.5 0.1 convert_reduce_fusion
  4.6 0.0 copy-start.7
  4.6 0.1 fusion.pick_ref
  4.8 0.6 dynamic_slice.25
  7.3 1.2 constant_dynamic-slice_fusion
  8.5 1.2 constant_dynamic-slice_fusion.2.hidden_later
  9.7 0.0 copy-done.2
  9.7 0.0 copy-done.1
  9.7 0.0 copy-start.8
  9.7 50.5 %shard_map.103 = (bf16[256,8192]{1,0:T(8,128)(2,1)}, bf16[256,256]{1,0:T(8,128)(2,1)S(1)}, bf16[256,1024]{1,0:T(8,128)(2,1)S(1)}, bf16[256,1024]{1,0:T(8,128)(2,1)S(1)}) custom-call(bf16[512,2048]{1,0:T(8,128)(2,1)} %hidden_hbm.1, bf16[512,1024]{1,0:T(8,128)(2,1)S(1)} %copy-done.1, bf16[512,1024]{1,0:T(8,128)(2,1)S(1)} %copy-done.2, ...), custom_call_target="tpu_custom_call" | custom-call | tf_op jit(solution)/shard_map/pallas_call | solution.py:323
  60.2 0.0 copy-start.3
  60.3 0.8 copy-done.3
  61.0 0.0 copy-start.4
  61.0 0.8 copy-done.4
  61.8 0.0 copy-start.5
  61.8 0.6 copy-done.5
  62.5 0.0 copy-done.8
  62.5 0.1 reshape.158
  62.6 0.1 select_reduce_fusion
  62.7 0.8 copy.13.scale_ref
  63.5 0.0 copy-done.7
  63.5 0.8 copy.14.seg_col_ref
  64.3 9.5 %shard_map.104 = (bf16[256,1024]{1,0:T(8,128)(2,1)}, bf16[256,256]{1,0:T(8,128)(2,1)}) custom-call(bf16[256,1024]{1,0:T(8,128)(2,1)} %copy-done.3, bf16[256,256]{1,0:T(8,128)(2,1)} %copy-done.5, bf16[256,256]{1,0:T(8,128)(2,1)} %copy-done.5, bf16[256,1024]{1,0:T(8,128)(2,1)} %copy-done.4, f32[256,1]{1,0:T(8,128)} %copy.13.scale_ref, ...), custom_call_target="tpu_custom_call" | custom-call | tf_op jit(solution)/shard_map/pallas_call | solution.py:119
  73.7 0.0 copy-start
  73.8 2.2 %copy-done = bf16[256,8192]{1,0:T(8,128)(2,1)S(1)} copy-done((bf16[256,8192]{1,0:T(8,128)(2,1)S(1)}, bf16[256,8192]{1,0:T(8,128)(2,1)}, u32[]{:S(2)}) %copy-start) | copy-done | bytes 4194328
  75.9 0.0 copy-start.6
  75.9 0.9 copy-done.6
  76.8 64.3 %shard_map.105 = (f32[1024,128]{1,0:T(8,128)S(1)}, f32[1024,128]{1,0:T(8,128)S(1)}) custom-call(bf16[256,8192]{1,0:T(8,128)(2,1)S(1)} %copy-done, bf16[256,256]{1,0:T(8,128)(2,1)S(1)} %copy-done.6), custom_call_target="tpu_custom_call" | custom-call | tf_op jit(solution)/shard_map/pallas_call | solution.py:443
  141.1 0.8 copy.17
  141.9 0.8 copy.18
  (9 shorter events, 0.1 us)
Async XLA Ops:
  0.6 9.1 %copy-start.2 = (bf16[512,1024]{1,0:T(8,128)(2,1)S(1)}, bf16[512,1024]{1,0:T(8,128)(2,1)}, u32[]{:S(2)}) copy-start(bf16[512,1024]{1,0:T(8,128)(2,1)} %upstream_hbm.1) | copy-start | bytes 3145732
  0.6 9.1 %copy-start.1 = (bf16[512,1024]{1,0:T(8,128)(2,1)S(1)}, bf16[512,1024]{1,0:T(8,128)(2,1)}, u32[]{:S(2)}) copy-start(bf16[512,1024]{1,0:T(8,128)(2,1)} %query_hbm.1) | copy-start | bytes 3145732
  4.6 58.9 %copy-start.7 = (s32[256]{0:T(256)}, s32[256]{0:T(256)S(1)}, u32[]{:S(2)}) copy-start(s32[256]{0:T(256)S(1)} %get-tuple-element.19) | copy-start | bytes 3076
  9.7 52.8 %copy-start.8 = (f32[8,8]{1,0:T(8,128)S(1)}, f32[8,8]{1,0:T(8,128)}, u32[]{:S(2)}) copy-start(f32[8,8]{1,0:T(8,128)} %param.14) | copy-start | bytes 772
  60.2 0.8 copy-start.3
  61.0 0.8 copy-start.4
  61.8 0.6 copy-start.5
  73.7 2.2 %copy-start = (bf16[256,8192]{1,0:T(8,128)(2,1)S(1)}, bf16[256,8192]{1,0:T(8,128)(2,1)}, u32[]{:S(2)}) copy-start(bf16[256,8192]{1,0:T(8,128)(2,1)} %get-tuple-element.15.normed_ref) | copy-start | bytes 12582916
  75.9 0.9 copy-start.6

commit v6 on v5

--- a/solution.py
+++ b/solution.py
@@ -13,7 +13,7 @@
 PIECE = 128
 LAST_START = CAP_R - PIECE
 CHUNKS = 4
-AHEAD = 3
+AHEAD = 2
 
 epsilon = 1e-06
 masked_score = -1e30

time: 144 us -> 144 us (level); the launches traced: 143 us -> 144 us
  Pallas kernels: 124 us -> 126 us
    pallas_call x1, Pallas kernels: 64.3 us -> 65.9 us  [gradient_sum(): pl.pallas_call(functools.partial(gradient_kernel, count), in_specs=[vmem,...]
where the time goes in v6:
time: 144 us
  Pallas kernels  126 us (88%)
  local copies, waits for them, and re-layouts  11.8 us (8%)
  other arithmetic  3.98 us (3%)
  between operations  2.72 us (2%)
    pallas_call x1, Pallas kernels, gradient_sum(): pl.pallas_call(functools.partial(gradient_kernel, count), in_specs=[vmem,...  65.9 us
    pallas_call x1, Pallas kernels, front(): pl.pallas_call(functools.partial(front_kernel, lax.axis_size('dp')), in_s...  50.5 us
    pallas_call x1, Pallas kernels, attend(): pl.pallas_call(attention_kernel, grid=(width // HD,), in_specs=[head_bloc...  9.47 us
    unnamed x20, local copies, waits for them, and re-layouts  6.92 us

profile of v6, /device:TPU:0, one launch (start us, length us, event | category | flops | bytes accessed | tf_op | source)
XLA Modules:
  0.0 144.3 jit_solution(13834387975338404361)
XLA Ops:
  0.6 0.0 copy-start.2
  0.6 0.0 copy-start.1
  0.7 0.9 convert_reduce_fusion.1
  1.6 0.1 select_add_fusion
  1.7 0.9 select_select_fusion
  2.6 0.8 multiply_reduce_fusion
  3.4 0.1 bitcast_subtract_fusion
  3.5 0.8 fusion.4
  4.2 0.1 broadcast_in_dim.86
  4.3 0.1 select_reduce_fusion.2
  4.4 0.1 reshape.157
  4.5 0.1 convert_reduce_fusion
  4.6 0.0 copy-start.7
  4.6 0.1 fusion.pick_ref
  4.8 0.6 dynamic_slice.25
  7.3 1.2 constant_dynamic-slice_fusion
  8.5 1.2 constant_dynamic-slice_fusion.2.hidden_later
  9.7 0.0 copy-done.2
  9.7 0.0 copy-done.1
  9.7 0.0 copy-start.8
  9.7 50.5 %shard_map.103 = (bf16[256,8192]{1,0:T(8,128)(2,1)}, bf16[256,256]{1,0:T(8,128)(2,1)S(1)}, bf16[256,1024]{1,0:T(8,128)(2,1)S(1)}, bf16[256,1024]{1,0:T(8,128)(2,1)S(1)}) custom-call(bf16[512,2048]{1,0:T(8,128)(2,1)} %hidden_hbm.1, bf16[512,1024]{1,0:T(8,128)(2,1)S(1)} %copy-done.1, bf16[512,1024]{1,0:T(8,128)(2,1)S(1)} %copy-done.2, ...), custom_call_target="tpu_custom_call" | custom-call | tf_op jit(solution)/shard_map/pallas_call | solution.py:323
  60.2 0.0 copy-start.3
  60.3 0.8 copy-done.3
  61.0 0.0 copy-start.4
  61.0 0.8 copy-done.4
  61.8 0.0 copy-start.5
  61.8 0.6 copy-done.5
  62.5 0.0 copy-done.8
  62.5 0.1 reshape.158
  62.6 0.1 select_reduce_fusion
  62.7 0.8 copy.13.scale_ref
  63.5 0.0 copy-done.7
  63.5 0.8 copy.14.seg_col_ref
  64.3 9.5 %shard_map.104 = (bf16[256,1024]{1,0:T(8,128)(2,1)}, bf16[256,256]{1,0:T(8,128)(2,1)}) custom-call(bf16[256,1024]{1,0:T(8,128)(2,1)} %copy-done.3, bf16[256,256]{1,0:T(8,128)(2,1)} %copy-done.5, bf16[256,256]{1,0:T(8,128)(2,1)} %copy-done.5, bf16[256,1024]{1,0:T(8,128)(2,1)} %copy-done.4, f32[256,1]{1,0:T(8,128)} %copy.13.scale_ref, ...), custom_call_target="tpu_custom_call" | custom-call | tf_op jit(solution)/shard_map/pallas_call | solution.py:119
  73.7 0.0 copy-start
  73.8 2.2 %copy-done = bf16[256,8192]{1,0:T(8,128)(2,1)S(1)} copy-done((bf16[256,8192]{1,0:T(8,128)(2,1)S(1)}, bf16[256,8192]{1,0:T(8,128)(2,1)}, u32[]{:S(2)}) %copy-start) | copy-done | bytes 4194328
  75.9 0.0 copy-start.6
  75.9 0.9 copy-done.6
  76.8 65.9 %shard_map.105 = (f32[1024,128]{1,0:T(8,128)S(1)}, f32[1024,128]{1,0:T(8,128)S(1)}) custom-call(bf16[256,8192]{1,0:T(8,128)(2,1)S(1)} %copy-done, bf16[256,256]{1,0:T(8,128)(2,1)S(1)} %copy-done.6), custom_call_target="tpu_custom_call" | custom-call | tf_op jit(solution)/shard_map/pallas_call | solution.py:443
  142.7 0.8 copy.17
  143.5 0.8 copy.18
  (9 shorter events, 0.1 us)
Async XLA Ops:
  0.6 9.1 %copy-start.2 = (bf16[512,1024]{1,0:T(8,128)(2,1)S(1)}, bf16[512,1024]{1,0:T(8,128)(2,1)}, u32[]{:S(2)}) copy-start(bf16[512,1024]{1,0:T(8,128)(2,1)} %upstream_hbm.1) | copy-start | bytes 3145732
  0.6 9.1 %copy-start.1 = (bf16[512,1024]{1,0:T(8,128)(2,1)S(1)}, bf16[512,1024]{1,0:T(8,128)(2,1)}, u32[]{:S(2)}) copy-start(bf16[512,1024]{1,0:T(8,128)(2,1)} %query_hbm.1) | copy-start | bytes 3145732
  4.6 58.9 %copy-start.7 = (s32[256]{0:T(256)}, s32[256]{0:T(256)S(1)}, u32[]{:S(2)}) copy-start(s32[256]{0:T(256)S(1)} %get-tuple-element.19) | copy-start | bytes 3076
  9.7 52.8 %copy-start.8 = (f32[8,8]{1,0:T(8,128)S(1)}, f32[8,8]{1,0:T(8,128)}, u32[]{:S(2)}) copy-start(f32[8,8]{1,0:T(8,128)} %param.14) | copy-start | bytes 772
  60.2 0.8 copy-start.3
  61.0 0.8 copy-start.4
  61.8 0.6 copy-start.5
  73.7 2.2 %copy-start = (bf16[256,8192]{1,0:T(8,128)(2,1)S(1)}, bf16[256,8192]{1,0:T(8,128)(2,1)}, u32[]{:S(2)}) copy-start(bf16[256,8192]{1,0:T(8,128)(2,1)} %get-tuple-element.15.normed_ref) | copy-start | bytes 12582916
  75.9 0.9 copy-start.6
